TPU v7x, 32 devices: a whole 2x2x4 slice. The times are simulated.
32 devices in a mesh: blk: 16 (over z, y, core), grp: 2 (over x).
Axes of the slice: x: 2, y: 2, z: 4, core: 2. Of those that a mesh axis runs over, the one named last changes fastest.
Arguments:
- tracers: float32 [2, 16, 128, 256], P(None, None, 'blk', 'grp'), may hold values from -6 to 6
- velocity: float32 [2, 16, 128, 256], P(None, None, 'blk', 'grp'), may hold values from -3 to 3
- depth_levels: int32 [128, 256], P('blk', 'grp'), may hold values from 0 to 16, as said below
- vdiff: float32 [15], replicated, may hold values from 0.05 to 0.45
Outputs:
- new_tracers: float32 [2, 16, 128, 256], P(None, None, 'blk', 'grp')
- surface: float32 [128, 256], P('blk', 'grp')
- residual: float32 [128, 256], P('blk', 'grp')
Inputs may be any that keep to these rules, and one draw needn't show every extreme that they name: `depth_levels`: 16 and 0 are both reached in every draw.
All inputs are finite; a program needn't handle non-finite values.
Results may differ from a plain program's by a relative error of at most 0.0003.
Values sent between devices are 32-bit elements; how exact they have to be, the bound alone decides.
No kernel may reach another device: no remote copies, remote signals or barrier semaphores. Data moves between devices by JAX's collectives and lax.ppermute only.
A program may use at most 64 MiB of HBM per device.

v0:
```python
import jax
import jax.numpy as jnp
from jax import lax
from jax.sharding import PartitionSpec as P

ITERS = 3


TIME_STEP = 0.2
MIX_COEF = 0.25
SEA_DIAG = 0.5


def swapped(value, axis, stride):
    return lax.ppermute(value, axis, [(i, i ^ 1 << stride) for i in range(lax.axis_size(axis))])


def padded_2(cells, sides, width, closed):
    for axis, dim in sides:
        count = lax.axis_size(axis)
        ends = count if closed else count - 1
        head = lax.slice_in_dim(cells, 0, width, axis=dim)
        tail = lax.slice_in_dim(cells, cells.shape[dim] - width, cells.shape[dim], axis=dim)
        cells = jnp.concatenate(
            [
                lax.ppermute(tail, axis, [(i, (i + 1) % count) for i in range(ends)]),
                cells,
                lax.ppermute(head, axis, [((i + 1) % count, i) for i in range(ends)]),
            ],
            axis=dim,
        )
    return cells


def tracer_step(tracer, velocity, depth_pad, vdiff):
    count = tracer.shape[1]
    levels = jnp.arange(count, dtype=jnp.float32)[:, None, None]
    wet_mask = (levels < depth_pad[None]).astype(jnp.float32)
    east_vel = velocity[0]
    north_vel = velocity[1]
    row_set = tracer[:, :, 1:-1, :]
    wet_rows = wet_mask[:, 1:-1, :]
    east_rows = east_vel[:, 1:-1, :]
    east_open = wet_rows[:, :, :-1] * wet_rows[:, :, 1:]
    east_face = 0.5 * (east_rows[:, :, :-1] + east_rows[:, :, 1:])
    east_flux = east_open * (
        east_face * 0.5 * (row_set[..., :-1] + row_set[..., 1:])
        - MIX_COEF * (row_set[..., 1:] - row_set[..., :-1])
    )
    col_set = tracer[:, :, :, 1:-1]
    wet_cols = wet_mask[:, :, 1:-1]
    north_cols = north_vel[:, :, 1:-1]
    north_open = wet_cols[:, :-1, :] * wet_cols[:, 1:, :]
    north_face = 0.5 * (north_cols[:, :-1, :] + north_cols[:, 1:, :])
    north_flux = north_open * (
        north_face * 0.5 * (col_set[:, :, :-1, :] + col_set[:, :, 1:, :])
        - MIX_COEF * (col_set[:, :, 1:, :] - col_set[:, :, :-1, :])
    )
    centre = tracer[:, :, 1:-1, 1:-1]
    wet_centre = wet_mask[:, 1:-1, 1:-1]
    vert_open = wet_centre[:-1] * wet_centre[1:]
    vert_flux = vdiff[:, None, None] * vert_open * (centre[:, 1:] - centre[:, :-1])
    border = jnp.zeros_like(centre[:, :1])
    vert_flux = jnp.concatenate([border, vert_flux, border], 1)
    tendency = (
        vert_flux[:, 1:]
        - vert_flux[:, :-1]
        - (east_flux[..., 1:] - east_flux[..., :-1])
        - (north_flux[:, :, 1:, :] - north_flux[:, :, :-1, :])
    )
    return wet_centre * (centre + TIME_STEP * tendency)


def column_forcing(velocity, depth_pad):
    count = velocity.shape[1]
    levels = jnp.arange(count, dtype=jnp.float32)[:, None, None]
    wet_mask = (levels < depth_pad[None]).astype(jnp.float32)
    east_sum = jnp.sum(wet_mask * velocity[0], 0)
    north_sum = jnp.sum(wet_mask * velocity[1], 0)
    ocean_mask = (depth_pad[1:-1, 1:-1] > 0).astype(jnp.float32)
    return ocean_mask * (
        0.5 * (east_sum[1:-1, 2:] - east_sum[1:-1, :-2])
        + 0.5 * (north_sum[2:, 1:-1] - north_sum[:-2, 1:-1])
    )


def sea_operator(field_pad, depth_pad, count):
    centre = field_pad[1:-1, 1:-1]
    depth_c = depth_pad[1:-1, 1:-1]
    ocean_mask = (depth_c > 0).astype(jnp.float32)
    total = SEA_DIAG * centre
    for rows_at, cols_at in (
        (slice(1, -1), slice(2, None)),
        (slice(1, -1), slice(None, -2)),
        (slice(2, None), slice(1, -1)),
        (slice(None, -2), slice(1, -1)),
    ):
        weight = jnp.minimum(depth_c, depth_pad[rows_at, cols_at]) / count
        total = total + weight * (centre - field_pad[rows_at, cols_at])
    return ocean_mask * total + (1.0 - ocean_mask) * centre


def extend(fields, fold_sign):
    top_row = fields[:, -1, :]
    partner = top_row
    for bit_index in range(lax.axis_size("grp").bit_length() - 1):
        partner = swapped(partner, "grp", bit_index)
    mirror = partner[:, ::-1]
    northmost = lax.axis_index("blk") == lax.axis_size("blk") - 1
    row_halo = padded_2(fields, (("blk", 1),), 1, False)
    north_row = jnp.where(northmost, mirror * fold_sign[:, None], row_halo[:, -1, :])
    grown = jnp.concatenate([row_halo[:, :-1, :], north_row[:, None, :]], 1)
    return padded_2(grown, (("grp", 2),), 1, True)


def two_sums(residual, applied):
    return lax.psum((jnp.sum(residual * residual), jnp.sum(residual * applied)), ("blk", "grp"))


def shards(tracers, velocity, depth_levels, vdiff):
    count = tracers.shape[1]
    height, breadth = depth_levels.shape
    fields = jnp.concatenate(
        [
            tracers.reshape(2 * count, height, breadth),
            velocity.reshape(2 * count, height, breadth),
            depth_levels.astype(jnp.float32)[None],
        ],
        0,
    )
    fold_sign = jnp.concatenate(
        [
            jnp.ones((2 * count,), jnp.float32),
            -jnp.ones((2 * count,), jnp.float32),
            jnp.ones((1,), jnp.float32),
        ]
    )
    padded = extend(fields, fold_sign)
    tracer_pad = padded[: 2 * count].reshape(2, count, height + 2, breadth + 2)
    velocity_pad = padded[2 * count : 4 * count].reshape(2, count, height + 2, breadth + 2)
    depth_pad = padded[4 * count]
    new_tracers = tracer_step(tracer_pad, velocity_pad, depth_pad, vdiff)
    forcing = column_forcing(velocity_pad, depth_pad)

    def apply_op(field):
        grown = extend(field[None], jnp.ones((1,), jnp.float32))[0]
        return sea_operator(grown, depth_pad, count)

    surface = jnp.zeros_like(forcing)
    residual = forcing
    applied = apply_op(residual)
    norm_now, product = two_sums(residual, applied)
    step_len = norm_now / product
    direction, along = (residual, applied)
    for sweep in range(ITERS):
        surface = surface + step_len * direction
        residual = residual - step_len * along
        if sweep + 1 < ITERS:
            applied = apply_op(residual)
            norm_next, product = two_sums(residual, applied)
            beta_ratio = norm_next / norm_now
            step_len = norm_next / (product - beta_ratio * norm_next / step_len)
            direction = residual + beta_ratio * direction
            along = applied + beta_ratio * along
            norm_now = norm_next
    return (new_tracers, surface, residual)


def solution(mesh):
    return jax.shard_map(
        shards,
        mesh=mesh,
        in_specs=(P(None, None, "blk", "grp"), P(None, None, "blk", "grp"), P("blk", "grp"), P()),
        out_specs=(P(None, None, "blk", "grp"), P("blk", "grp"), P("blk", "grp")),
        check_vma=False,
    )
```

profile of v0, /device:TPU:5, one launch (start us, length us, event | category | flops | bytes accessed | tf_op | source)
XLA Modules:
  0.0 195.9 jit_solution(13682118741915809105)
XLA Ops:
  1.3 1.1 pad_maximum_fusion.20
  2.5 1.3 collective-permute-start.1
  3.8 2.9 %collective-permute-start.2 = (f32[65,1,128]{2,0,1:T(8,128)S(1)}, f32[65,1,128]{2,0,1:T(8,128)S(1)}, u32[]{:S(2)}, u32[]{:S(2)}) collective-permute-start(f32[65,1,128]{2,0,1:T(8,128)S(1)} %copy.46), channel_id=1, source_target_pairs={{2,0},{4,2},{6,4},{8,6},{10,8},{12,10},{14,12},{16,14},{18,16},{20... | collective-permute-start | bytes 99848 | tf_op jit(solution)/shard_map/ppermute | solution.py:28
  6.6 3.6 %collective-permute-start = (f32[65,1,128]{2,1,0:T(1,128)S(1)}, f32[65,1,128]{2,1,0:T(1,128)S(1)}, u32[]{:S(2)}, u32[]{:S(2)}) collective-permute-start(f32[65,1,128]{2,1,0:T(1,128)S(1)} %get-tuple-element.27), channel_id=1, source_target_pairs={{0,2},{2,4},{4,6},{6,8},{8,10},{10,12},{12,14},{14,16},{16,18},{18... | collective-permute-start | bytes 99848 | tf_op jit(solution)/shard_map/ppermute | solution.py:26
  11.2 1.1 pad_maximum_fusion.1
  13.2 1.2 collective-permute-start.3
  14.5 1.2 collective-permute-done.3
  17.3 6.6 %collective-permute-start.5 = (f32[1,1,128]{2,1,0:T(1,128)S(1)}, f32[1,1,128]{2,1,0:T(1,128)S(1)}, u32[]{:S(2)}, u32[]{:S(2)}) collective-permute-start(f32[1,1,128]{2,1,0:T(1,128)S(1)} %get-tuple-element.43), channel_id=1, source_target_pairs={{0,2},{2,4},{4,6},{6,8},{8,10},{10,12},{12,14},{14,16},{16,18},{18... | collective-permute-start | bytes 1544 | tf_op jit(solution)/shard_map/ppermute | solution.py:26
  23.8 1.3 collective-permute-start.6
  25.1 1.9 collective-permute-start.7
  29.1 1.7 collective-permute-done.7
  31.2 1.2 collective-permute-start.9
  32.5 1.0 collective-permute-done.8
  34.5 40.5 %all-reduce.4 = (f32[]{:T(128)}, f32[]{:T(128)}) all-reduce(f32[]{:T(128)} %get-tuple-element.13, f32[]{:T(128)} %get-tuple-element.12), channel_id=1, replica_groups=mesh['blk'=16,'grp'=2] {'blk','grp'}, use_global_device_ids=true, to_apply=%region_3.4 | all-reduce | flops 2 | bytes 16 | tf_op jit(solution)/shard_map/psum | solution.py:117
  76.6 4.6 %collective-permute-start.12 = (f32[1,1,128]{2,1,0:T(1,128)S(1)}, f32[1,1,128]{2,1,0:T(1,128)S(1)}, u32[]{:S(2)}, u32[]{:S(2)}) collective-permute-start(f32[1,1,128]{2,1,0:T(1,128)S(1)} %get-tuple-element.42), channel_id=1, source_target_pairs={{2,0},{4,2},{6,4},{8,6},{10,8},{12,10},{14,12},{16,14},{18,16},{20... | collective-permute-start | bytes 1544 | tf_op jit(solution)/shard_map/ppermute | solution.py:28
  81.5 2.8 %collective-permute-start.10 = (f32[1,1,128]{2,1,0:T(1,128)S(1)}, f32[1,1,128]{2,1,0:T(1,128)S(1)}, u32[]{:S(2)}, u32[]{:S(2)}) collective-permute-start(f32[1,1,128]{2,1,0:T(1,128)S(1)} %get-tuple-element.40), channel_id=1, source_target_pairs={{0,2},{2,4},{4,6},{6,8},{8,10},{10,12},{12,14},{14,16},{16,18},{18... | collective-permute-start | bytes 1544 | tf_op jit(solution)/shard_map/ppermute | solution.py:26
  85.4 1.2 collective-permute-start.14
  86.6 1.0 collective-permute-done.13
  88.6 42.6 %all-reduce.3 = (f32[]{:T(128)}, f32[]{:T(128)}) all-reduce(f32[]{:T(128)} %get-tuple-element.11, f32[]{:T(128)} %get-tuple-element.10), channel_id=1, replica_groups=mesh['blk'=16,'grp'=2] {'blk','grp'}, use_global_device_ids=true, to_apply=%region_7.8 | all-reduce | flops 2 | bytes 16 | tf_op jit(solution)/shard_map/psum | solution.py:117
  136.5 4.4 %collective-permute-start.17 = (f32[1,1,128]{2,1,0:T(1,128)S(1)}, f32[1,1,128]{2,1,0:T(1,128)S(1)}, u32[]{:S(2)}, u32[]{:S(2)}) collective-permute-start(f32[1,1,128]{2,1,0:T(1,128)S(1)} %get-tuple-element.39), channel_id=1, source_target_pairs={{2,0},{4,2},{6,4},{8,6},{10,8},{12,10},{14,12},{16,14},{18,16},{20... | collective-permute-start | bytes 1544 | tf_op jit(solution)/shard_map/ppermute | solution.py:28
  141.8 2.7 %collective-permute-start.15 = (f32[1,1,128]{2,1,0:T(1,128)S(1)}, f32[1,1,128]{2,1,0:T(1,128)S(1)}, u32[]{:S(2)}, u32[]{:S(2)}) collective-permute-start(f32[1,1,128]{2,1,0:T(1,128)S(1)} %get-tuple-element.37), channel_id=1, source_target_pairs={{0,2},{2,4},{4,6},{6,8},{8,10},{10,12},{12,14},{14,16},{16,18},{18... | collective-permute-start | bytes 1544 | tf_op jit(solution)/shard_map/ppermute | solution.py:26
  145.6 1.1 collective-permute-start.19
  146.7 1.0 collective-permute-done.18
  148.9 42.3 %all-reduce.2 = (f32[]{:T(128)}, f32[]{:T(128)}) all-reduce(f32[]{:T(128)} %get-tuple-element.9, f32[]{:T(128)} %get-tuple-element.8), channel_id=1, replica_groups=mesh['blk'=16,'grp'=2] {'blk','grp'}, use_global_device_ids=true, to_apply=%region_11.12 | all-reduce | flops 2 | bytes 16 | tf_op jit(solution)/shard_map/psum | solution.py:117
  (86 shorter events, 14.5 us)
Async XLA Ops:
  2.5 7.8 %collective-permute-start.1 = (f32[65,128]{1,0:T(8,128)S(1)}, f32[65,128]{1,0:T(8,128)S(1)}, u32[]{:S(2)}, u32[]{:S(2)}) collective-permute-start(f32[65,128]{1,0:T(8,128)S(1)} %bitcast.70), channel_id=1, source_target_pairs={{0,1},{1,0},{2,3},{3,2},{4,5},{5,4},{6,7},{7,6},{8,9},{9,8},{10,11... | collective-permute-start | bytes 99848 | tf_op jit(solution)/shard_map/ppermute | solution.py:15
  3.8 6.6 %collective-permute-start.2 = (f32[65,1,128]{2,0,1:T(8,128)S(1)}, f32[65,1,128]{2,0,1:T(8,128)S(1)}, u32[]{:S(2)}, u32[]{:S(2)}) collective-permute-start(f32[65,1,128]{2,0,1:T(8,128)S(1)} %copy.46), channel_id=1, source_target_pairs={{2,0},{4,2},{6,4},{8,6},{10,8},{12,10},{14,12},{16,14},{18,16},{20... | collective-permute-start | bytes 99848 | tf_op jit(solution)/shard_map/ppermute | solution.py:28
  6.6 4.6 %collective-permute-start = (f32[65,1,128]{2,1,0:T(1,128)S(1)}, f32[65,1,128]{2,1,0:T(1,128)S(1)}, u32[]{:S(2)}, u32[]{:S(2)}) collective-permute-start(f32[65,1,128]{2,1,0:T(1,128)S(1)} %get-tuple-element.27), channel_id=1, source_target_pairs={{0,2},{2,4},{4,6},{6,8},{8,10},{10,12},{12,14},{14,16},{16,18},{18... | collective-permute-start | bytes 99848 | tf_op jit(solution)/shard_map/ppermute | solution.py:26
  12.5 1.9 copy-start
  12.5 1.9 copy-start.1
  12.9 3.1 %collective-permute-start.4 = (f32[65,10,1]{0,2,1:T(1,128)S(1)}, f32[65,10,1]{0,2,1:T(1,128)S(1)}, u32[]{:S(2)}, u32[]{:S(2)}) collective-permute-start(f32[65,10,1]{0,2,1:T(1,128)S(1)} %copy.31), channel_id=1, source_target_pairs={{1,0},{0,1},{3,2},{2,3},{5,4},{4,5},{7,6},{6,7},{9,8},{8,9},{11,10... | collective-permute-start | bytes 7808 | tf_op jit(solution)/shard_map/ppermute | solution.py:28
  13.2 2.5 %collective-permute-start.3 = (f32[65,10,1]{0,2,1:T(1,128)S(1)}, f32[65,10,1]{0,2,1:T(1,128)S(1)}, u32[]{:S(2)}, u32[]{:S(2)}) collective-permute-start(f32[65,10,1]{0,2,1:T(1,128)S(1)} %copy.30), channel_id=1, source_target_pairs={{0,1},{1,0},{2,3},{3,2},{4,5},{5,4},{6,7},{7,6},{8,9},{9,8},{10,11... | collective-permute-start | bytes 7808 | tf_op jit(solution)/shard_map/ppermute | solution.py:26
  17.3 13.6 %collective-permute-start.5 = (f32[1,1,128]{2,1,0:T(1,128)S(1)}, f32[1,1,128]{2,1,0:T(1,128)S(1)}, u32[]{:S(2)}, u32[]{:S(2)}) collective-permute-start(f32[1,1,128]{2,1,0:T(1,128)S(1)} %get-tuple-element.43), channel_id=1, source_target_pairs={{0,2},{2,4},{4,6},{6,8},{8,10},{10,12},{12,14},{14,16},{16,18},{18... | collective-permute-start | bytes 1544 | tf_op jit(solution)/shard_map/ppermute | solution.py:26
  23.8 5.2 %collective-permute-start.6 = (f32[1,128]{1,0:T(1,128)S(1)}, f32[1,128]{1,0:T(1,128)S(1)}, u32[]{:S(2)}, u32[]{:S(2)}) collective-permute-start(f32[1,128]{1,0:T(1,128)S(1)} %get-tuple-element.44), channel_id=1, source_target_pairs={{0,1},{1,0},{2,3},{3,2},{4,5},{5,4},{6,7},{7,6},{8,9},{9,8},{10,11... | collective-permute-start | bytes 1544 | tf_op jit(solution)/shard_map/ppermute | solution.py:15
  25.1 5.8 %collective-permute-start.7 = (f32[1,1,128]{2,1,0:T(1,128)S(1)}, f32[1,1,128]{2,1,0:T(1,128)S(1)}, u32[]{:S(2)}, u32[]{:S(2)}) collective-permute-start(f32[1,1,128]{2,1,0:T(1,128)S(1)} %get-tuple-element.45), channel_id=1, source_target_pairs={{2,0},{4,2},{6,4},{8,6},{10,8},{12,10},{14,12},{16,14},{18,16},{20... | collective-permute-start | bytes 1544 | tf_op jit(solution)/shard_map/ppermute | solution.py:28
  28.2 0.7 copy-start.2
  31.0 2.5 %collective-permute-start.8 = (f32[1,10,1]{2,1,0:T(8,128)S(1)}, f32[1,10,1]{2,1,0:T(8,128)S(1)}, u32[]{:S(2)}, u32[]{:S(2)}) collective-permute-start(f32[1,10,1]{2,1,0:T(8,128)S(1)} %get-tuple-element.33), channel_id=1, source_target_pairs={{0,1},{1,0},{2,3},{3,2},{4,5},{5,4},{6,7},{7,6},{8,9},{9,8},{10,11... | collective-permute-start | bytes 128 | tf_op jit(solution)/shard_map/ppermute | solution.py:26
  31.2 2.5 %collective-permute-start.9 = (f32[1,10,1]{2,1,0:T(8,128)S(1)}, f32[1,10,1]{2,1,0:T(8,128)S(1)}, u32[]{:S(2)}, u32[]{:S(2)}) collective-permute-start(f32[1,10,1]{2,1,0:T(8,128)S(1)} %get-tuple-element.34), channel_id=1, source_target_pairs={{1,0},{0,1},{3,2},{2,3},{5,4},{4,5},{7,6},{6,7},{9,8},{8,9},{11,10... | collective-permute-start | bytes 128 | tf_op jit(solution)/shard_map/ppermute | solution.py:28
  76.3 8.0 %collective-permute-start.11 = (f32[1,128]{1,0:T(1,128)S(1)}, f32[1,128]{1,0:T(1,128)S(1)}, u32[]{:S(2)}, u32[]{:S(2)}) collective-permute-start(f32[1,128]{1,0:T(1,128)S(1)} %get-tuple-element.41), channel_id=1, source_target_pairs={{0,1},{1,0},{2,3},{3,2},{4,5},{5,4},{6,7},{7,6},{8,9},{9,8},{10,11... | collective-permute-start | bytes 1544 | tf_op jit(solution)/shard_map/ppermute | solution.py:15
  76.6 7.8 %collective-permute-start.12 = (f32[1,1,128]{2,1,0:T(1,128)S(1)}, f32[1,1,128]{2,1,0:T(1,128)S(1)}, u32[]{:S(2)}, u32[]{:S(2)}) collective-permute-start(f32[1,1,128]{2,1,0:T(1,128)S(1)} %get-tuple-element.42), channel_id=1, source_target_pairs={{2,0},{4,2},{6,4},{8,6},{10,8},{12,10},{14,12},{16,14},{18,16},{20... | collective-permute-start | bytes 1544 | tf_op jit(solution)/shard_map/ppermute | solution.py:28
  81.5 3.5 %collective-permute-start.10 = (f32[1,1,128]{2,1,0:T(1,128)S(1)}, f32[1,1,128]{2,1,0:T(1,128)S(1)}, u32[]{:S(2)}, u32[]{:S(2)}) collective-permute-start(f32[1,1,128]{2,1,0:T(1,128)S(1)} %get-tuple-element.40), channel_id=1, source_target_pairs={{0,2},{2,4},{4,6},{6,8},{8,10},{10,12},{12,14},{14,16},{16,18},{18... | collective-permute-start | bytes 1544 | tf_op jit(solution)/shard_map/ppermute | solution.py:26
  85.1 2.5 %collective-permute-start.13 = (f32[1,10,1]{2,1,0:T(8,128)S(1)}, f32[1,10,1]{2,1,0:T(8,128)S(1)}, u32[]{:S(2)}, u32[]{:S(2)}) collective-permute-start(f32[1,10,1]{2,1,0:T(8,128)S(1)} %get-tuple-element.31), channel_id=1, source_target_pairs={{0,1},{1,0},{2,3},{3,2},{4,5},{5,4},{6,7},{7,6},{8,9},{9,8},{10,11... | collective-permute-start | bytes 128 | tf_op jit(solution)/shard_map/ppermute | solution.py:26
  85.4 2.5 %collective-permute-start.14 = (f32[1,10,1]{2,1,0:T(8,128)S(1)}, f32[1,10,1]{2,1,0:T(8,128)S(1)}, u32[]{:S(2)}, u32[]{:S(2)}) collective-permute-start(f32[1,10,1]{2,1,0:T(8,128)S(1)} %get-tuple-element.32), channel_id=1, source_target_pairs={{1,0},{0,1},{3,2},{2,3},{5,4},{4,5},{7,6},{6,7},{9,8},{8,9},{11,10... | collective-permute-start | bytes 128 | tf_op jit(solution)/shard_map/ppermute | solution.py:28
  136.0 8.5 %collective-permute-start.16 = (f32[1,128]{1,0:T(1,128)S(1)}, f32[1,128]{1,0:T(1,128)S(1)}, u32[]{:S(2)}, u32[]{:S(2)}) collective-permute-start(f32[1,128]{1,0:T(1,128)S(1)} %get-tuple-element.38), channel_id=1, source_target_pairs={{0,1},{1,0},{2,3},{3,2},{4,5},{5,4},{6,7},{7,6},{8,9},{9,8},{10,11... | collective-permute-start | bytes 1544 | tf_op jit(solution)/shard_map/ppermute | solution.py:15
  136.5 8.1 %collective-permute-start.17 = (f32[1,1,128]{2,1,0:T(1,128)S(1)}, f32[1,1,128]{2,1,0:T(1,128)S(1)}, u32[]{:S(2)}, u32[]{:S(2)}) collective-permute-start(f32[1,1,128]{2,1,0:T(1,128)S(1)} %get-tuple-element.39), channel_id=1, source_target_pairs={{2,0},{4,2},{6,4},{8,6},{10,8},{12,10},{14,12},{16,14},{18,16},{20... | collective-permute-start | bytes 1544 | tf_op jit(solution)/shard_map/ppermute | solution.py:28
  141.8 3.4 %collective-permute-start.15 = (f32[1,1,128]{2,1,0:T(1,128)S(1)}, f32[1,1,128]{2,1,0:T(1,128)S(1)}, u32[]{:S(2)}, u32[]{:S(2)}) collective-permute-start(f32[1,1,128]{2,1,0:T(1,128)S(1)} %get-tuple-element.37), channel_id=1, source_target_pairs={{0,2},{2,4},{4,6},{6,8},{8,10},{10,12},{12,14},{14,16},{16,18},{18... | collective-permute-start | bytes 1544 | tf_op jit(solution)/shard_map/ppermute | solution.py:26
  145.2 2.5 %collective-permute-start.18 = (f32[1,10,1]{2,1,0:T(8,128)S(1)}, f32[1,10,1]{2,1,0:T(8,128)S(1)}, u32[]{:S(2)}, u32[]{:S(2)}) collective-permute-start(f32[1,10,1]{2,1,0:T(8,128)S(1)} %get-tuple-element.29), channel_id=1, source_target_pairs={{0,1},{1,0},{2,3},{3,2},{4,5},{5,4},{6,7},{7,6},{8,9},{9,8},{10,11... | collective-permute-start | bytes 128 | tf_op jit(solution)/shard_map/ppermute | solution.py:26
  145.6 2.5 %collective-permute-start.19 = (f32[1,10,1]{2,1,0:T(8,128)S(1)}, f32[1,10,1]{2,1,0:T(8,128)S(1)}, u32[]{:S(2)}, u32[]{:S(2)}) collective-permute-start(f32[1,10,1]{2,1,0:T(8,128)S(1)} %get-tuple-element.30), channel_id=1, source_target_pairs={{1,0},{0,1},{3,2},{2,3},{5,4},{4,5},{7,6},{6,7},{9,8},{8,9},{11,10... | collective-permute-start | bytes 128 | tf_op jit(solution)/shard_map/ppermute | solution.py:28
where the time goes:
time: 198 us; the launch traced here: 196 us
  blocking collectives  125 us (63%)
  starting transfers between devices  38.7 us (20%)
  between operations  11.1 us (6%)
  other arithmetic  9.03 us (5%)
  waiting for transfers between devices  8.27 us (4%)
  local copies, waits for them, and re-layouts  3.44 us (2%)
    psum x3, blocking collectives, two_sums(): lax.psum((jnp.sum(residual * residual), jnp.sum(residual * applied)), ('b...  125 us
    ppermute x8, starting transfers between devices, padded_2(): lax.ppermute(tail, axis, [(i, (i + 1) % count) for i in range(ends)])  17.8 us
    ppermute x8, starting transfers between devices, padded_2(): lax.ppermute(head, axis, [((i + 1) % count, i) for i in range(ends)])  17.6 us
    ppermute x8, waiting for transfers between devices, padded_2(): lax.ppermute(tail, axis, [(i, (i + 1) % count) for i in range(ends)])  5.59 us
  transfers between devices with their start and end apart: 20, of which 11 were waited for; matrix products, arithmetic and copies ran while one was open for 2% of the time, Pallas kernels for 0%

commit v1 on v0

--- a/solution.py
+++ b/solution.py
@@ -1,6 +1,10 @@
+import functools
+
 import jax
 import jax.numpy as jnp
 from jax import lax
+from jax.experimental import pallas as pl
+from jax.experimental.pallas import tpu as pltpu
 from jax.sharding import PartitionSpec as P
 
 ITERS = 3
@@ -9,6 +13,9 @@
 TIME_STEP = 0.2
 MIX_COEF = 0.25
 SEA_DIAG = 0.5
+
+AXES = ("blk", "grp")
+GATHER_CELLS = 1 << 17
 
 
 def swapped(value, axis, stride):
@@ -114,10 +121,10 @@
 
 
 def two_sums(residual, applied):
-    return lax.psum((jnp.sum(residual * residual), jnp.sum(residual * applied)), ("blk", "grp"))
-
-
-def shards(tracers, velocity, depth_levels, vdiff):
+    return lax.psum((jnp.sum(residual * residual), jnp.sum(residual * applied)), AXES)
+
+
+def wide_shards(tracers, velocity, depth_levels, vdiff):
     count = tracers.shape[1]
     height, breadth = depth_levels.shape
     fields = jnp.concatenate(
@@ -166,6 +173,316 @@
     return (new_tracers, surface, residual)
 
 
+SUB, LANE = 8, 128
+
+
+def tile_iota(dim):
+    return lax.broadcasted_iota(jnp.int32, (SUB, LANE), dim)
+
+
+def reversed_lanes(value):
+    index = LANE - 1 - lax.broadcasted_iota(jnp.int32, value.shape, 1)
+    return jnp.take_along_axis(value, index, axis=1)
+
+
+def pack_kernel(count, tracers_ref, velocity_ref, depth_ref, sums_ref, low_ref, high_ref, edge_ref):
+    depth = depth_ref[...]
+    east = jnp.zeros((SUB, LANE), jnp.float32)
+    north = jnp.zeros((SUB, LANE), jnp.float32)
+    for level in range(count):
+        wet = depth > level
+        east += jnp.where(wet, velocity_ref[pl.ds(level * SUB, SUB), :], 0.0)
+        north += jnp.where(wet, velocity_ref[pl.ds((count + level) * SUB, SUB), :], 0.0)
+    depth_f = depth.astype(jnp.float32)
+    sums_ref[0:SUB, :] = east
+    sums_ref[SUB : 2 * SUB, :] = north
+    sums_ref[2 * SUB : 3 * SUB, :] = depth_f
+    for out_ref, row in ((low_ref, 0), (high_ref, SUB - 1)):
+        out_ref[0 : 2 * count, :] = tracers_ref[pl.ds(row, 2 * count, stride=SUB), :]
+        out_ref[2 * count : 3 * count, :] = velocity_ref[pl.ds(count * SUB + row, count, stride=SUB), :]
+        out_ref[3 * count : 3 * count + SUB, :] = jnp.broadcast_to(depth_f[row : row + 1, :], (SUB, LANE))
+    lane = tile_iota(1)
+    west_pack = jnp.zeros((SUB, LANE), jnp.float32)
+    east_pack = jnp.zeros((SUB, LANE), jnp.float32)
+    for field in range(3 * count + 1):
+        if field < 2 * count:
+            tile = tracers_ref[pl.ds(field * SUB, SUB), :]
+        elif field < 3 * count:
+            tile = velocity_ref[pl.ds((field - 2 * count) * SUB, SUB), :]
+        else:
+            tile = depth_f
+        west_pack = jnp.where(lane == field, pltpu.roll(tile, field, 1), west_pack)
+        east_pack = jnp.where(lane == field, pltpu.roll(tile, field + 1, 1), east_pack)
+    edge_ref[0:SUB, :] = west_pack
+    edge_ref[SUB : 2 * SUB, :] = east_pack
+
+
+def tracer_kernel(
+    count, blocks, place_ref, vdiff_ref, tracers_ref, velocity_ref, depth_ref, core_ref, far_ref, edge_ref, out_ref
+):
+    blk = place_ref[0] // 2
+    odd = (blk % 2) == 1
+    fold = blk == blocks - 1
+    lane, sub = tile_iota(1), tile_iota(0)
+    rows = core_ref.shape[0]
+    near = core_ref[...]
+    far = far_ref[...]
+    row_id = lax.broadcasted_iota(jnp.int32, (rows, LANE), 0)
+    sign = jnp.where((row_id >= 2 * count) & (row_id < 3 * count), -1.0, 1.0)
+    far_north = jnp.where(fold, reversed_lanes(far) * sign, far)
+    north_rows = jnp.where(odd, far_north, near)
+    south_rows = jnp.where(odd, near, far)
+    edge_base = edge_ref.shape[0] - 2 * SUB
+    east_cols = edge_ref[edge_base : edge_base + SUB, :]
+    west_cols = edge_ref[edge_base + SUB : edge_base + 2 * SUB, :]
+
+    def spread(packed, field, at):
+        return pltpu.roll(packed, (at - field) % LANE, 1)
+
+    def east_of(tile, field):
+        return jnp.where(lane == LANE - 1, spread(east_cols, field, LANE - 1), pltpu.roll(tile, LANE - 1, 1))
+
+    def west_of(tile, field):
+        return jnp.where(lane == 0, spread(west_cols, field, 0), pltpu.roll(tile, 1, 1))
+
+    def north_of(tile, field):
+        ghost = jnp.broadcast_to(north_rows[field : field + 1, :], (SUB, LANE))
+        return jnp.where(sub == SUB - 1, ghost, pltpu.roll(tile, SUB - 1, 0))
+
+    def south_of(tile, field):
+        ghost = jnp.broadcast_to(south_rows[field : field + 1, :], (SUB, LANE))
+        return jnp.where(sub == 0, ghost, pltpu.roll(tile, 1, 0))
+
+    depth = depth_ref[...].astype(jnp.float32)
+    at = 3 * count
+    open_east = jnp.minimum(depth, east_of(depth, at))
+    open_west = jnp.minimum(depth, west_of(depth, at))
+    open_north = jnp.minimum(depth, north_of(depth, at))
+    open_south = jnp.minimum(depth, south_of(depth, at))
+
+    def flux(here, there, speed):
+        return speed * (there + here) - MIX_COEF * (there - here)
+
+    below = [None, None]
+    for level in range(count):
+        u = velocity_ref[pl.ds(level * SUB, SUB), :]
+        v = velocity_ref[pl.ds((count + level) * SUB, SUB), :]
+        k = float(level)
+        east_speed = 0.25 * (u + east_of(u, 2 * count + level))
+        west_speed = 0.25 * (u + west_of(u, 2 * count + level))
+        north_speed = 0.25 * (v + north_of(v, 2 * count + level))
+        south_speed = 0.25 * (v + south_of(v, 2 * count + level))
+        for which in range(2):
+            field = which * count + level
+            here = tracers_ref[pl.ds(field * SUB, SUB), :]
+            out = jnp.where(open_east > k, flux(here, east_of(here, field), east_speed), 0.0)
+            out -= jnp.where(open_west > k, flux(west_of(here, field), here, west_speed), 0.0)
+            out += jnp.where(open_north > k, flux(here, north_of(here, field), north_speed), 0.0)
+            out -= jnp.where(open_south > k, flux(south_of(here, field), here, south_speed), 0.0)
+            tendency = -out
+            if level + 1 < count:
+                under = tracers_ref[pl.ds((field + 1) * SUB, SUB), :]
+                vertical = jnp.where(depth > k + 1.0, vdiff_ref[level] * (under - here), 0.0)
+                tendency += vertical
+            else:
+                vertical = None
+            if below[which] is not None:
+                tendency -= below[which]
+            below[which] = vertical
+            out_ref[pl.ds(field * SUB, SUB), :] = jnp.where(depth > k, here + TIME_STEP * tendency, 0.0)
+
+
+def solve_kernel(count, blocks, order, place_ref, own_ref, other_ref, surface_ref, residual_ref, fields, scratch):
+    me = place_ref[0]
+    core = (me // 2) % 2
+    height = blocks * SUB
+
+    for blk in range(blocks):
+        for grp in range(2):
+            apart = (blk * 2 + grp) ^ me
+            slot = 0
+            for bit, at in enumerate(order):
+                slot = slot + ((apart >> at) & 1) * (1 << bit)
+            mine = core == (blk % 2)
+            for part in range(3):
+                value = jnp.where(
+                    mine,
+                    own_ref[slot, part * SUB : (part + 1) * SUB, :],
+                    other_ref[slot, part * SUB : (part + 1) * SUB, :],
+                )
+                fields[part, grp, blk * SUB : (blk + 1) * SUB, :] = value
+
+    shape = (height, LANE)
+    lane = lax.broadcasted_iota(jnp.int32, shape, 1)
+    sub = tile_iota(0)
+
+    def east_of(pair):
+        low, high = (pltpu.roll(half, LANE - 1, 1) for half in pair)
+        return jnp.where(lane == LANE - 1, high, low), jnp.where(lane == LANE - 1, low, high)
+
+    def west_of(pair):
+        low, high = (pltpu.roll(half, 1, 1) for half in pair)
+        return jnp.where(lane == 0, high, low), jnp.where(lane == 0, low, high)
+
+    def north_of(pair, sign=1.0):
+        out = []
+        for half, mirror in zip(pair, pair[::-1]):
+            moved = pltpu.roll(half, height - 1, 0)
+            ghost = reversed_lanes(mirror[height - SUB :, :]) * sign
+            top = jnp.where(sub == SUB - 1, ghost, moved[height - SUB :, :])
+            out.append(jnp.concatenate([moved[: height - SUB, :], top], 0))
+        return tuple(out)
+
+    def south_of(pair):
+        out = []
+        for half in pair:
+            moved = pltpu.roll(half, 1, 0)
+            bottom = jnp.where(sub == 0, 0.0, moved[:SUB, :])
+            out.append(jnp.concatenate([bottom, moved[SUB:, :]], 0))
+        return tuple(out)
+
+    u = (fields[0, 0], fields[0, 1])
+    v = (fields[1, 0], fields[1, 1])
+    depth = (fields[2, 0], fields[2, 1])
+    weight_east = tuple(jnp.minimum(a, b) * (1.0 / count) for a, b in zip(depth, east_of(depth)))
+    weight_north = tuple(jnp.minimum(a, b) * (1.0 / count) for a, b in zip(depth, north_of(depth)))
+    diagonal = tuple(jnp.where(d > 0.0, SEA_DIAG, 1.0) for d in depth)
+
+    ue, uw, vn, vs = east_of(u), west_of(u), north_of(v, -1.0), south_of(v)
+    forcing = tuple(
+        jnp.where(depth[i] > 0.0, 0.5 * (ue[i] - uw[i]) + 0.5 * (vn[i] - vs[i]), 0.0) for i in range(2)
+    )
+
+    def apply_op(x):
+        xe, xn = east_of(x), north_of(x)
+        flux_e = tuple(weight_east[i] * (xe[i] - x[i]) for i in range(2))
+        flux_n = tuple(weight_north[i] * (xn[i] - x[i]) for i in range(2))
+        fw, fs = west_of(flux_e), south_of(flux_n)
+        return tuple(diagonal[i] * x[i] - (flux_e[i] - fw[i]) - (flux_n[i] - fs[i]) for i in range(2))
+
+    def total(a, b):
+        part = a[0] * b[0] + a[1] * b[1]
+        return jnp.sum(jnp.sum(part.reshape(blocks, SUB, LANE), 0), keepdims=True)
+
+    grp = me % 2
+    mine = pl.ds(pl.multiple_of((me // 2) * SUB, SUB), SUB)
+
+    def own(pair):
+        scratch[0] = pair[0]
+        scratch[1] = pair[1]
+        return jnp.where(grp == 0, scratch[0, mine, :], scratch[1, mine, :])
+
+    residual = forcing
+    applied = apply_op(residual)
+    norm_now, product = total(residual, residual), total(residual, applied)
+    step_len = norm_now / product
+    along = applied
+    own_residual = own(residual)
+    own_along = own(applied)
+    own_direction = own_residual
+    own_surface = jnp.zeros((SUB, LANE), jnp.float32)
+    for sweep in range(ITERS):
+        own_surface = own_surface + step_len * own_direction
+        own_residual = own_residual - step_len * own_along
+        if sweep + 1 < ITERS:
+            residual = tuple(residual[i] - step_len * along[i] for i in range(2))
+            applied = apply_op(residual)
+            norm_next, product = total(residual, residual), total(residual, applied)
+            beta_ratio = norm_next / norm_now
+            step_len = norm_next / (product - beta_ratio * norm_next / step_len)
+            own_direction = own_residual + beta_ratio * own_direction
+            own_along = own(applied) + beta_ratio * own_along
+            if sweep + 2 < ITERS:
+                along = tuple(applied[i] + beta_ratio * along[i] for i in range(2))
+            norm_now = norm_next
+    surface_ref[...] = own_surface
+    residual_ref[...] = own_residual
+
+
+VMEM_SPEC = pl.BlockSpec(memory_space=pltpu.VMEM)
+SMEM_SPEC = pl.BlockSpec(memory_space=pltpu.SMEM)
+
+
+def tile_shape(rows):
+    return jax.ShapeDtypeStruct((rows, LANE), jnp.float32)
+
+
+def small_shards(tracers, velocity, depth_levels, vdiff):
+    count = tracers.shape[1]
+    blocks = lax.axis_size("blk")
+    devices = blocks * 2
+    tracer_rows = tracers.reshape(2 * count * SUB, LANE)
+    velocity_rows = velocity.reshape(2 * count * SUB, LANE)
+    place = (lax.axis_index("blk") * 2 + lax.axis_index("grp")).astype(jnp.int32)
+    odd = lax.axis_index("blk") % 2 == 1
+
+    halo_rows = 3 * count + SUB
+    sums, low, high, edges = pl.pallas_call(
+        functools.partial(pack_kernel, count),
+        out_shape=[tile_shape(3 * SUB), tile_shape(halo_rows), tile_shape(halo_rows), tile_shape(2 * SUB)],
+        in_specs=[VMEM_SPEC] * 3,
+        out_specs=[VMEM_SPEC] * 4,
+        name="pack",
+    )(tracer_rows, velocity_rows, depth_levels)
+
+    near = lax.ppermute(jnp.where(odd, low, high), AXES, [(i, i ^ 2) for i in range(devices)])
+    far_pairs = []
+    for blk in range(1, blocks, 2):
+        for grp in range(2):
+            here = blk * 2 + grp
+            there = here ^ 1 if blk == blocks - 1 else here + 2
+            far_pairs.append((here, there))
+            if blk < blocks - 1:
+                far_pairs.append((there, here))
+    far = lax.ppermute(jnp.where(odd, high, low), AXES, far_pairs)
+
+    top = devices.bit_length() - 1
+    order = [bit for bit in range(top - 1, 2, -1)] + [0, 2]
+    gathered = sums
+    edge_pack = None
+    for bit in order:
+        pairs = [(i, i ^ 1 << bit) for i in range(devices)]
+        if bit == 0:
+            both = lax.ppermute(jnp.concatenate([gathered, edges], 0), AXES, pairs)
+            edge_pack = both
+            gathered = jnp.concatenate([gathered, both[: gathered.shape[0]]], 0)
+        else:
+            gathered = jnp.concatenate([gathered, lax.ppermute(gathered, AXES, pairs)], 0)
+    other = lax.ppermute(gathered, AXES, [(i, i ^ 2) for i in range(devices)])
+    slots = devices // 2
+
+    place_arr = place.reshape(1)
+    new_rows = pl.pallas_call(
+        functools.partial(tracer_kernel, count, blocks),
+        out_shape=tile_shape(2 * count * SUB),
+        in_specs=[SMEM_SPEC, SMEM_SPEC] + [VMEM_SPEC] * 6,
+        out_specs=VMEM_SPEC,
+        name="tracer",
+    )(place_arr, vdiff, tracer_rows, velocity_rows, depth_levels, near, far, edge_pack)
+
+    surface, residual = pl.pallas_call(
+        functools.partial(solve_kernel, count, blocks, tuple(order)),
+        out_shape=[tile_shape(SUB), tile_shape(SUB)],
+        in_specs=[SMEM_SPEC] + [VMEM_SPEC] * 2,
+        out_specs=[VMEM_SPEC] * 2,
+        scratch_shapes=[
+            pltpu.VMEM((3, 2, blocks * SUB, LANE), jnp.float32),
+            pltpu.VMEM((2, blocks * SUB, LANE), jnp.float32),
+        ],
+        name="solve",
+    )(place_arr, gathered.reshape(slots, 3 * SUB, LANE), other.reshape(slots, 3 * SUB, LANE))
+    return new_rows.reshape(tracers.shape), surface, residual
+
+
+def shards(tracers, velocity, depth_levels, vdiff):
+    blocks, groups = lax.axis_size("blk"), lax.axis_size("grp")
+    height, breadth = depth_levels.shape
+    tiled = (height, breadth) == (SUB, LANE) and groups == 2 and blocks >= 4 and blocks & (blocks - 1) == 0
+    if tiled and 3 * tracers.shape[1] < LANE and blocks * groups * SUB * LANE <= GATHER_CELLS:
+        return small_shards(tracers, velocity, depth_levels, vdiff)
+    return wide_shards(tracers, velocity, depth_levels, vdiff)
+
+
 def solution(mesh):
     return jax.shard_map(
         shards,

time: 198 us -> 34.6 us (0.17)
  blocking collectives: 125 us -> 0 us
  starting transfers between devices: 38.7 us -> 14.3 us
  between operations: 11.1 us -> 0.71 us
  other arithmetic: 9.03 us -> 0.02 us
  Pallas kernels: 0 us -> 6.46 us
    psum x3 -> x0, blocking collectives: 125 us -> none  [two_sums(): lax.psum((jnp.sum(residual * residual), jnp.sum(residual * applied)), ('b...]
    ppermute x20 -> x7, starting transfers between devices: 38.7 us -> 14.3 us  [the longest x1 5.35 us: small_shards(): other = lax.ppermute(gathered, AXES, [(i, i ^ 2) for i in range(devices)])]
    pallas_call x0 -> x3, Pallas kernels: none -> 6.46 us  [the longest x1 2.75 us: small_shards(): pl.pallas_call(functools.partial(solve_kernel, count, blocks, tuple(order...]
    reduce_sum x4 -> x0, other arithmetic: 2.49 us -> none  [the longest x3 2.08 us: two_sums(): jnp.sum(residual * applied)]
    ppermute x20 -> x7, waiting for transfers between devices: 8.27 us -> 10.1 us  [the longest x3 5.24 us: small_shards(): lax.ppermute(gathered, AXES, pairs)]
  transfers between devices with their start and end apart: 20 -> 7, of which waited for: 11 -> 5; matrix products, arithmetic and copies ran while one was open for 2% -> 2% of each run, Pallas kernels for 0% -> 6%
where the time goes in v1:
time: 34.6 us; the launch traced here: 34.3 us
  starting transfers between devices  14.3 us (41%)
  waiting for transfers between devices  10.1 us (29%)
  Pallas kernels  6.46 us (19%)
  local copies, waits for them, and re-layouts  2.66 us (8%)
  between operations  0.71 us (2%)
    ppermute x1, starting transfers between devices, small_shards(): other = lax.ppermute(gathered, AXES, [(i, i ^ 2) for i in range(devices)])  5.35 us
    ppermute x3, waiting for transfers between devices, small_shards(): lax.ppermute(gathered, AXES, pairs)  5.24 us
    ppermute x3, starting transfers between devices, small_shards(): lax.ppermute(gathered, AXES, pairs)  3.96 us
    ppermute x1, waiting for transfers between devices, small_shards(): far = lax.ppermute(jnp.where(odd, high, low), AXES, far_pairs)  3.02 us
    ppermute x1, starting transfers between devices, small_shards(): far = lax.ppermute(jnp.where(odd, high, low), AXES, far_pairs)  3.02 us
    pallas_call x1, Pallas kernels, small_shards(): pl.pallas_call(functools.partial(solve_kernel, count, blocks, tuple(order...  2.75 us
    unnamed x21, local copies, waits for them, and re-layouts  2.64 us
    pallas_call x1, Pallas kernels, small_shards(): pl.pallas_call(functools.partial(tracer_kernel, count, blocks), out_shape...  1.97 us
  transfers between devices with their start and end apart: 7, of which 5 were waited for; matrix products, arithmetic and copies ran while one was open for 2% of the time, Pallas kernels for 6%

profile of v1, /device:TPU:5, one launch (start us, length us, event | category | flops | bytes accessed | tf_op | source)
XLA Modules:
  0.0 34.3 jit_solution(18023757271362225614)
XLA Ops:
  0.6 1.7 %pack.1 = (f32[24,128]{1,0:T(8,128)}, f32[56,128]{1,0:T(8,128)}, f32[56,128]{1,0:T(8,128)}, f32[16,128]{1,0:T(8,128)}) custom-call(f32[256,128]{1,0:T(8,128)} %bitcast.6, f32[256,128]{1,0:T(8,128)} %bitcast.8, s32[8,128]{1,0:T(8,128)} %depth_ref.3), custom_call_target="tpu_custom_call" | custom-call | tf_op jit(solution)/shard_map/pack/pallas_call | solution.py:420
  2.4 2.3 %collective-permute-start.2 = (f32[24,128]{1,0:T(8,128)}, f32[24,128]{1,0:T(8,128)S(1)}, u32[]{:S(2)}, u32[]{:S(2)}) collective-permute-start(f32[24,128]{1,0:T(8,128)} %get-tuple-element.11), channel_id=1, source_target_pairs={{0,16},{1,17},{2,18},{3,19},{4,20},{5,21},{6,22},{7,23},{8,24},{9,... | collective-permute-start | bytes 36872 | tf_op jit(solution)/shard_map/ppermute | solution.py:450
  4.7 0.7 %constant_dynamic-update-slice_fusion.4 = f32[384,128]{1,0:T(8,128)S(1)} fusion(f32[24,128]{1,0:T(8,128)} %get-tuple-element.11), kind=kLoop, calls=%fused_computation.9 | loop fusion | bytes 24576
  5.4 0.6 %collective-permute-done.2 = f32[24,128]{1,0:T(8,128)S(1)} collective-permute-done((f32[24,128]{1,0:T(8,128)}, f32[24,128]{1,0:T(8,128)S(1)}, u32[]{:S(2)}, u32[]{:S(2)}) %collective-permute-start.2) | collective-permute-done | bytes 12320 | tf_op jit(solution)/shard_map/ppermute | solution.py:450
  6.0 0.0 copy-done.3
  6.1 1.4 %collective-permute-start.3 = (f32[48,128]{1,0:T(8,128)S(1)}, f32[48,128]{1,0:T(8,128)S(1)}, u32[]{:S(2)}, u32[]{:S(2)}) collective-permute-start(f32[48,128]{1,0:T(8,128)S(1)} %pad_maximum_fusion.2), channel_id=1, source_target_pairs={{0,8},{1,9},{2,10},{3,11},{4,12},{5,13},{6,14},{7,15},{8,0},{9,1},... | collective-permute-start | bytes 73736 | tf_op jit(solution)/shard_map/ppermute | solution.py:450
  7.4 1.4 %collective-permute-done.3 = f32[48,128]{1,0:T(8,128)S(1)} collective-permute-done((f32[48,128]{1,0:T(8,128)S(1)}, f32[48,128]{1,0:T(8,128)S(1)}, u32[]{:S(2)}, u32[]{:S(2)}) %collective-permute-start.3) | collective-permute-done | bytes 24608 | tf_op jit(solution)/shard_map/ppermute | solution.py:450
  8.8 0.0 copy-done.8
  8.8 1.3 %collective-permute-start.4 = (f32[112,128]{1,0:T(8,128)S(1)}, f32[112,128]{1,0:T(8,128)S(1)}, u32[]{:S(2)}, u32[]{:S(2)}) collective-permute-start(f32[112,128]{1,0:T(8,128)S(1)} %pad_maximum_fusion.1), channel_id=1, source_target_pairs={{0,1},{1,0},{2,3},{3,2},{4,5},{5,4},{6,7},{7,6},{8,9},{9,8},{10,11... | collective-permute-start | bytes 172040 | tf_op jit(solution)/shard_map/ppermute | solution.py:446
  10.1 1.8 %collective-permute-done.4.edge_ref = f32[112,128]{1,0:T(8,128)S(1)} collective-permute-done((f32[112,128]{1,0:T(8,128)S(1)}, f32[112,128]{1,0:T(8,128)S(1)}, u32[]{:S(2)}, u32[]{:S(2)}) %collective-permute-start.4) | collective-permute-done | bytes 57376 | tf_op jit(solution)/shard_map/ppermute | solution.py:446
  11.9 0.6 %copy-done.1 = f32[112,128]{1,0:T(8,128)} copy-done((f32[112,128]{1,0:T(8,128)}, f32[112,128]{1,0:T(8,128)S(1)}, u32[]{:S(2)}) %copy-start.1) | copy-done | bytes 57368
  12.5 0.3 collective-permute-start.5
  12.8 3.2 %collective-permute-done.5 = f32[192,128]{1,0:T(8,128)S(1)} collective-permute-done((f32[192,128]{1,0:T(8,128)S(1)}, f32[192,128]{1,0:T(8,128)S(1)}, u32[]{:S(2)}, u32[]{:S(2)}) %collective-permute-start.5) | collective-permute-done | bytes 98336 | tf_op jit(solution)/shard_map/ppermute | solution.py:450
  16.1 5.3 %collective-permute-start.6 = (f32[384,128]{1,0:T(8,128)S(1)}, f32[384,128]{1,0:T(8,128)S(1)}, u32[]{:S(2)}, u32[]{:S(2)}) collective-permute-start(f32[384,128]{1,0:T(8,128)S(1)} %constant_dynamic-update-slice_fusion), channel_id=1, source_target_pairs={{0,2},{1,3},{2,0},{3,1},{4,6},{5,7},{6,4},{7,5},{8,10},{9,11},{10,... | collective-permute-start | bytes 589832 | tf_op jit(solution)/shard_map/ppermute | solution.py:451
  21.4 0.7 %collective-permute-start = (f32[56,128]{1,0:T(8,128)S(1)}, f32[56,128]{1,0:T(8,128)S(1)}, u32[]{:S(2)}, u32[]{:S(2)}) collective-permute-start(f32[56,128]{1,0:T(8,128)S(1)} %get-tuple-element.18), channel_id=1, source_target_pairs={{0,2},{1,3},{2,0},{3,1},{4,6},{5,7},{6,4},{7,5},{8,10},{9,11},{10,... | collective-permute-start | bytes 86024 | tf_op jit(solution)/shard_map/ppermute | solution.py:428
  22.2 3.0 %collective-permute-start.1 = (f32[56,128]{1,0:T(8,128)S(1)}, f32[56,128]{1,0:T(8,128)S(1)}, u32[]{:S(2)}, u32[]{:S(2)}) collective-permute-start(f32[56,128]{1,0:T(8,128)S(1)} %get-tuple-element.17), channel_id=1, source_target_pairs={{2,4},{4,2},{3,5},{5,3},{6,8},{8,6},{7,9},{9,7},{10,12},{12,10},{1... | collective-permute-start | bytes 86024 | tf_op jit(solution)/shard_map/ppermute | solution.py:437
  25.2 0.0 collective-permute-done.core_ref
  25.2 0.0 copy-start.6
  25.2 3.0 %collective-permute-done.1.far_ref = f32[56,128]{1,0:T(8,128)S(1)} collective-permute-done((f32[56,128]{1,0:T(8,128)S(1)}, f32[56,128]{1,0:T(8,128)S(1)}, u32[]{:S(2)}, u32[]{:S(2)}) %collective-permute-start.1) | collective-permute-done | bytes 28704 | tf_op jit(solution)/shard_map/ppermute | solution.py:437
  28.2 0.6 %copy-done.7 = f32[56,128]{1,0:T(8,128)} copy-done((f32[56,128]{1,0:T(8,128)}, f32[56,128]{1,0:T(8,128)S(1)}, u32[]{:S(2)}) %copy-start.7) | copy-done | bytes 28696
  28.9 2.0 %tracer.1 = f32[256,128]{1,0:T(8,128)} custom-call(s32[1]{0:T(128)} %bitcast.place_ref, f32[15]{0:T(128)} %vdiff_ref.1, f32[256,128]{1,0:T(8,128)} %bitcast.7, f32[256,128]{1,0:T(8,128)} %bitcast.9, s32[8,128]{1,0:T(8,128)} %depth_ref.3, f32[56,128]{1,0:T(8,128)} %copy-done.6, f32[56,128]{1,0:T(8,128)} %copy-done.7, f32[112,128]{1,0:T(8,128)} %copy-done.1), custom_call_target="tpu_custom_call" | custom-call | tf_op jit(solution)/shard_map/tracer/pallas_call | solution.py:455
  30.8 0.0 collective-permute-done.6
  30.8 0.7 %copy-done.2 = f32[384,128]{1,0:T(8,128)} copy-done((f32[384,128]{1,0:T(8,128)}, f32[384,128]{1,0:T(8,128)S(1)}, u32[]{:S(2)}) %copy-start.2) | copy-done | bytes 196632
  31.5 2.7 %solve.1 = (f32[8,128]{1,0:T(8,128)}, f32[8,128]{1,0:T(8,128)}) custom-call(s32[1]{0:T(128)} %bitcast.place_ref, f32[16,24,128]{2,1,0:T(8,128)} %bitcast.10, f32[16,24,128]{2,1,0:T(8,128)} %bitcast.11), custom_call_target="tpu_custom_call" | custom-call | tf_op jit(solution)/shard_map/solve/pallas_call | solution.py:463
  (20 shorter events, 0.1 us)
Async XLA Ops:
  2.4 3.7 %copy-start.3 = (f32[24,128]{1,0:T(8,128)S(1)}, f32[24,128]{1,0:T(8,128)}, u32[]{:S(2)}) copy-start(f32[24,128]{1,0:T(8,128)} %get-tuple-element.11) | copy-start | bytes 36868
  2.4 3.7 %collective-permute-start.2 = (f32[24,128]{1,0:T(8,128)}, f32[24,128]{1,0:T(8,128)S(1)}, u32[]{:S(2)}, u32[]{:S(2)}) collective-permute-start(f32[24,128]{1,0:T(8,128)} %get-tuple-element.11), channel_id=1, source_target_pairs={{0,16},{1,17},{2,18},{3,19},{4,20},{5,21},{6,22},{7,23},{8,24},{9,... | collective-permute-start | bytes 36872 | tf_op jit(solution)/shard_map/ppermute | solution.py:450
  6.1 2.8 %copy-start.8 = (f32[16,128]{1,0:T(8,128)S(1)}, f32[16,128]{1,0:T(8,128)}, u32[]{:S(2)}) copy-start(f32[16,128]{1,0:T(8,128)} %get-tuple-element.12) | copy-start | bytes 24580
  6.1 2.7 %collective-permute-start.3 = (f32[48,128]{1,0:T(8,128)S(1)}, f32[48,128]{1,0:T(8,128)S(1)}, u32[]{:S(2)}, u32[]{:S(2)}) collective-permute-start(f32[48,128]{1,0:T(8,128)S(1)} %pad_maximum_fusion.2), channel_id=1, source_target_pairs={{0,8},{1,9},{2,10},{3,11},{4,12},{5,13},{6,14},{7,15},{8,0},{9,1},... | collective-permute-start | bytes 73736 | tf_op jit(solution)/shard_map/ppermute | solution.py:450
  8.8 3.1 %collective-permute-start.4 = (f32[112,128]{1,0:T(8,128)S(1)}, f32[112,128]{1,0:T(8,128)S(1)}, u32[]{:S(2)}, u32[]{:S(2)}) collective-permute-start(f32[112,128]{1,0:T(8,128)S(1)} %pad_maximum_fusion.1), channel_id=1, source_target_pairs={{0,1},{1,0},{2,3},{3,2},{4,5},{5,4},{6,7},{7,6},{8,9},{9,8},{10,11... | collective-permute-start | bytes 172040 | tf_op jit(solution)/shard_map/ppermute | solution.py:446
  11.9 0.6 %copy-start.1 = (f32[112,128]{1,0:T(8,128)}, f32[112,128]{1,0:T(8,128)S(1)}, u32[]{:S(2)}) copy-start(f32[112,128]{1,0:T(8,128)S(1)} %collective-permute-done.4.edge_ref) | copy-start | bytes 172036
  12.5 3.5 %collective-permute-start.5 = (f32[192,128]{1,0:T(8,128)S(1)}, f32[192,128]{1,0:T(8,128)S(1)}, u32[]{:S(2)}, u32[]{:S(2)}) collective-permute-start(f32[192,128]{1,0:T(8,128)S(1)} %pad_maximum_fusion), channel_id=1, source_target_pairs={{0,4},{1,5},{2,6},{3,7},{4,0},{5,1},{6,2},{7,3},{8,12},{9,13},{10,... | collective-permute-start | bytes 294920 | tf_op jit(solution)/shard_map/ppermute | solution.py:450
  16.1 5.4 %copy-start.4 = (f32[56,128]{1,0:T(8,128)S(1)}, f32[56,128]{1,0:T(8,128)}, u32[]{:S(2)}) copy-start(f32[56,128]{1,0:T(8,128)} %get-tuple-element.9) | copy-start | bytes 86020
  16.1 5.4 %copy-start.5 = (f32[56,128]{1,0:T(8,128)S(1)}, f32[56,128]{1,0:T(8,128)}, u32[]{:S(2)}) copy-start(f32[56,128]{1,0:T(8,128)} %get-tuple-element.10) | copy-start | bytes 86020
  16.1 14.8 %copy-start = (f32[384,128]{1,0:T(8,128)}, f32[384,128]{1,0:T(8,128)S(1)}, u32[]{:S(2)}) copy-start(f32[384,128]{1,0:T(8,128)S(1)} %constant_dynamic-update-slice_fusion) | copy-start | bytes 589828
  16.1 14.7 %collective-permute-start.6 = (f32[384,128]{1,0:T(8,128)S(1)}, f32[384,128]{1,0:T(8,128)S(1)}, u32[]{:S(2)}, u32[]{:S(2)}) collective-permute-start(f32[384,128]{1,0:T(8,128)S(1)} %constant_dynamic-update-slice_fusion), channel_id=1, source_target_pairs={{0,2},{1,3},{2,0},{3,1},{4,6},{5,7},{6,4},{7,5},{8,10},{9,11},{10,... | collective-permute-start | bytes 589832 | tf_op jit(solution)/shard_map/ppermute | solution.py:451
  21.4 3.8 %collective-permute-start = (f32[56,128]{1,0:T(8,128)S(1)}, f32[56,128]{1,0:T(8,128)S(1)}, u32[]{:S(2)}, u32[]{:S(2)}) collective-permute-start(f32[56,128]{1,0:T(8,128)S(1)} %get-tuple-element.18), channel_id=1, source_target_pairs={{0,2},{1,3},{2,0},{3,1},{4,6},{5,7},{6,4},{7,5},{8,10},{9,11},{10,... | collective-permute-start | bytes 86024 | tf_op jit(solution)/shard_map/ppermute | solution.py:428
  22.2 6.1 %collective-permute-start.1 = (f32[56,128]{1,0:T(8,128)S(1)}, f32[56,128]{1,0:T(8,128)S(1)}, u32[]{:S(2)}, u32[]{:S(2)}) collective-permute-start(f32[56,128]{1,0:T(8,128)S(1)} %get-tuple-element.17), channel_id=1, source_target_pairs={{2,4},{4,2},{3,5},{5,3},{6,8},{8,6},{7,9},{9,7},{10,12},{12,10},{1... | collective-permute-start | bytes 86024 | tf_op jit(solution)/shard_map/ppermute | solution.py:437
  25.2 3.0 %copy-start.6 = (f32[56,128]{1,0:T(8,128)}, f32[56,128]{1,0:T(8,128)S(1)}, u32[]{:S(2)}) copy-start(f32[56,128]{1,0:T(8,128)S(1)} %collective-permute-done.core_ref) | copy-start | bytes 86020
  28.2 0.6 %copy-start.7 = (f32[56,128]{1,0:T(8,128)}, f32[56,128]{1,0:T(8,128)S(1)}, u32[]{:S(2)}) copy-start(f32[56,128]{1,0:T(8,128)S(1)} %collective-permute-done.1.far_ref) | copy-start | bytes 86020
  30.8 0.7 %copy-start.2 = (f32[384,128]{1,0:T(8,128)}, f32[384,128]{1,0:T(8,128)S(1)}, u32[]{:S(2)}) copy-start(f32[384,128]{1,0:T(8,128)S(1)} %collective-permute-done.6) | copy-start | bytes 589828

commit v2 on v1

--- a/solution.py
+++ b/solution.py
@@ -6,6 +6,7 @@
 from jax.experimental import pallas as pl
 from jax.experimental.pallas import tpu as pltpu
 from jax.sharding import PartitionSpec as P
+
 
 ITERS = 3
 
@@ -185,7 +186,20 @@
     return jnp.take_along_axis(value, index, axis=1)
 
 
-def pack_kernel(count, tracers_ref, velocity_ref, depth_ref, sums_ref, low_ref, high_ref, edge_ref):
+def pack_kernel(
+    count, tracers_hbm, velocity_hbm, depth_hbm, sums_ref, near_ref, far_ref, tracers_ref, velocity_ref, depth_ref, sems
+):
+    copies = [
+        pltpu.make_async_copy(src, dst, sems.at[at])
+        for at, (src, dst) in enumerate(
+            ((depth_hbm, depth_ref), (velocity_hbm, velocity_ref), (tracers_hbm, tracers_ref))
+        )
+    ]
+    for copy in copies:
+        copy.start()
+    odd = lax.axis_index("blk") % 2 == 1
+    copies[0].wait()
+    copies[1].wait()
     depth = depth_ref[...]
     east = jnp.zeros((SUB, LANE), jnp.float32)
     north = jnp.zeros((SUB, LANE), jnp.float32)
@@ -197,10 +211,25 @@
     sums_ref[0:SUB, :] = east
     sums_ref[SUB : 2 * SUB, :] = north
     sums_ref[2 * SUB : 3 * SUB, :] = depth_f
-    for out_ref, row in ((low_ref, 0), (high_ref, SUB - 1)):
-        out_ref[0 : 2 * count, :] = tracers_ref[pl.ds(row, 2 * count, stride=SUB), :]
-        out_ref[2 * count : 3 * count, :] = velocity_ref[pl.ds(count * SUB + row, count, stride=SUB), :]
-        out_ref[3 * count : 3 * count + SUB, :] = jnp.broadcast_to(depth_f[row : row + 1, :], (SUB, LANE))
+    copies[2].wait()
+
+    def both(ref, first, rows):
+        low = ref[pl.ds(first, rows, stride=SUB), :]
+        high = ref[pl.ds(first + SUB - 1, rows, stride=SUB), :]
+        return jnp.where(odd, low, high), jnp.where(odd, high, low)
+
+    depth_low = jnp.broadcast_to(depth_f[0:1, :], (SUB, LANE))
+    depth_high = jnp.broadcast_to(depth_f[SUB - 1 : SUB, :], (SUB, LANE))
+    parts = (
+        both(tracers_ref, 0, 2 * count),
+        both(velocity_ref, count * SUB, count),
+        (jnp.where(odd, depth_low, depth_high), jnp.where(odd, depth_high, depth_low)),
+    )
+    at = 0
+    for near, far in parts:
+        near_ref[at : at + near.shape[0], :] = near
+        far_ref[at : at + near.shape[0], :] = far
+        at += near.shape[0]
     lane = tile_iota(1)
     west_pack = jnp.zeros((SUB, LANE), jnp.float32)
     east_pack = jnp.zeros((SUB, LANE), jnp.float32)
@@ -213,20 +242,20 @@
             tile = depth_f
         west_pack = jnp.where(lane == field, pltpu.roll(tile, field, 1), west_pack)
         east_pack = jnp.where(lane == field, pltpu.roll(tile, field + 1, 1), east_pack)
-    edge_ref[0:SUB, :] = west_pack
-    edge_ref[SUB : 2 * SUB, :] = east_pack
+    near_ref[at : at + SUB, :] = west_pack
+    near_ref[at + SUB : at + 2 * SUB, :] = east_pack
 
 
 def tracer_kernel(
-    count, blocks, place_ref, vdiff_ref, tracers_ref, velocity_ref, depth_ref, core_ref, far_ref, edge_ref, out_ref
+    count, blocks, vdiff_ref, tracers_ref, velocity_ref, depth_ref, near_ref, far_ref, edge_ref, out_ref
 ):
-    blk = place_ref[0] // 2
-    odd = (blk % 2) == 1
+    blk = lax.axis_index("blk")
+    odd = blk % 2 == 1
     fold = blk == blocks - 1
     lane, sub = tile_iota(1), tile_iota(0)
-    rows = core_ref.shape[0]
-    near = core_ref[...]
-    far = far_ref[...]
+    rows = far_ref.shape[0]
+    near = near_ref[0:rows, :]
+    far = jnp.where(blk == 0, 0.0, far_ref[...])
     row_id = lax.broadcasted_iota(jnp.int32, (rows, LANE), 0)
     sign = jnp.where((row_id >= 2 * count) & (row_id < 3 * count), -1.0, 1.0)
     far_north = jnp.where(fold, reversed_lanes(far) * sign, far)
@@ -292,25 +321,25 @@
             out_ref[pl.ds(field * SUB, SUB), :] = jnp.where(depth > k, here + TIME_STEP * tendency, 0.0)
 
 
-def solve_kernel(count, blocks, order, place_ref, own_ref, other_ref, surface_ref, residual_ref, fields, scratch):
-    me = place_ref[0]
-    core = (me // 2) % 2
+def solve_kernel(count, blocks, order, own_ref, other_ref, surface_ref, residual_ref, scratch):
+    me = lax.axis_index("blk") * 2 + lax.axis_index("grp")
     height = blocks * SUB
 
-    for blk in range(blocks):
-        for grp in range(2):
-            apart = (blk * 2 + grp) ^ me
-            slot = 0
-            for bit, at in enumerate(order):
-                slot = slot + ((apart >> at) & 1) * (1 << bit)
-            mine = core == (blk % 2)
-            for part in range(3):
-                value = jnp.where(
-                    mine,
-                    own_ref[slot, part * SUB : (part + 1) * SUB, :],
-                    other_ref[slot, part * SUB : (part + 1) * SUB, :],
-                )
-                fields[part, grp, blk * SUB : (blk + 1) * SUB, :] = value
+    def slot_of(place):
+        return sum(((place >> at) & 1) << bit for bit, at in enumerate(order))
+
+    def core_of(place):
+        return sum((place >> at) & 1 for at in (*order, 1)) & 1
+
+    my_slot, my_core = slot_of(me), core_of(me)
+
+    def tile(part, place):
+        rows = slice(part * SUB, (part + 1) * SUB)
+        slot = slot_of(place) ^ my_slot
+        return jnp.where(my_core == core_of(place), own_ref[slot, rows, :], other_ref[slot, rows, :])
+
+    def field(part):
+        return tuple(jnp.concatenate([tile(part, blk * 2 + grp) for blk in range(blocks)], 0) for grp in range(2))
 
     shape = (height, LANE)
     lane = lax.broadcasted_iota(jnp.int32, shape, 1)
@@ -341,9 +370,7 @@
             out.append(jnp.concatenate([bottom, moved[SUB:, :]], 0))
         return tuple(out)
 
-    u = (fields[0, 0], fields[0, 1])
-    v = (fields[1, 0], fields[1, 1])
-    depth = (fields[2, 0], fields[2, 1])
+    u, v, depth = field(0), field(1), field(2)
     weight_east = tuple(jnp.minimum(a, b) * (1.0 / count) for a, b in zip(depth, east_of(depth)))
     weight_north = tuple(jnp.minimum(a, b) * (1.0 / count) for a, b in zip(depth, north_of(depth)))
     diagonal = tuple(jnp.where(d > 0.0, SEA_DIAG, 1.0) for d in depth)
@@ -401,6 +428,7 @@
 
 VMEM_SPEC = pl.BlockSpec(memory_space=pltpu.VMEM)
 SMEM_SPEC = pl.BlockSpec(memory_space=pltpu.SMEM)
+SMALL_GRANT = pltpu.CompilerParams(vmem_limit_bytes=8 << 20)
 
 
 def tile_shape(rows):
@@ -411,66 +439,65 @@
     count = tracers.shape[1]
     blocks = lax.axis_size("blk")
     devices = blocks * 2
-    tracer_rows = tracers.reshape(2 * count * SUB, LANE)
-    velocity_rows = velocity.reshape(2 * count * SUB, LANE)
-    place = (lax.axis_index("blk") * 2 + lax.axis_index("grp")).astype(jnp.int32)
-    odd = lax.axis_index("blk") % 2 == 1
-
+    rows = 2 * count * SUB
     halo_rows = 3 * count + SUB
-    sums, low, high, edges = pl.pallas_call(
+
+    sums, near, far, tracer_rows, velocity_rows, depth = pl.pallas_call(
         functools.partial(pack_kernel, count),
-        out_shape=[tile_shape(3 * SUB), tile_shape(halo_rows), tile_shape(halo_rows), tile_shape(2 * SUB)],
-        in_specs=[VMEM_SPEC] * 3,
-        out_specs=[VMEM_SPEC] * 4,
+        out_shape=[
+            tile_shape(3 * SUB),
+            tile_shape(halo_rows + 2 * SUB),
+            tile_shape(halo_rows),
+            tile_shape(rows),
+            tile_shape(rows),
+            jax.ShapeDtypeStruct((SUB, LANE), jnp.int32),
+        ],
+        in_specs=[pl.BlockSpec(memory_space=pltpu.HBM)] * 3,
+        out_specs=[VMEM_SPEC] * 6,
+        scratch_shapes=[pltpu.SemaphoreType.DMA((3,))],
+        compiler_params=SMALL_GRANT,
         name="pack",
-    )(tracer_rows, velocity_rows, depth_levels)
-
-    near = lax.ppermute(jnp.where(odd, low, high), AXES, [(i, i ^ 2) for i in range(devices)])
+    )(*(pltpu.with_memory_space_constraint(x, pltpu.HBM) for x in (tracers.reshape(rows, LANE), velocity.reshape(rows, LANE), depth_levels)))
+
+    near = lax.ppermute(near, AXES, [(i, i ^ 2) for i in range(devices)])
     far_pairs = []
     for blk in range(1, blocks, 2):
         for grp in range(2):
             here = blk * 2 + grp
-            there = here ^ 1 if blk == blocks - 1 else here + 2
-            far_pairs.append((here, there))
-            if blk < blocks - 1:
-                far_pairs.append((there, here))
-    far = lax.ppermute(jnp.where(odd, high, low), AXES, far_pairs)
-
-    top = devices.bit_length() - 1
-    order = [bit for bit in range(top - 1, 2, -1)] + [0, 2]
-    gathered = sums
-    edge_pack = None
+            far_pairs += [(here, here ^ 1)] if blk == blocks - 1 else [(here, here + 2), (here + 2, here)]
+    far = lax.ppermute(far, AXES, far_pairs + [(0, 1), (1, 0)])
+
+    order = [*range(devices.bit_length() - 2, 2, -1), 0, 2]
+    gathered, edges = sums, None
     for bit in order:
-        pairs = [(i, i ^ 1 << bit) for i in range(devices)]
+        pairs = [(i, i ^ (1 << bit | 2)) for i in range(devices)]
         if bit == 0:
-            both = lax.ppermute(jnp.concatenate([gathered, edges], 0), AXES, pairs)
-            edge_pack = both
-            gathered = jnp.concatenate([gathered, both[: gathered.shape[0]]], 0)
+            edges = lax.ppermute(jnp.concatenate([gathered, near[halo_rows:]], 0), AXES, pairs)
+            came = edges[: gathered.shape[0]]
         else:
-            gathered = jnp.concatenate([gathered, lax.ppermute(gathered, AXES, pairs)], 0)
+            came = lax.ppermute(gathered, AXES, pairs)
+        gathered = jnp.concatenate([gathered, came], 0)
     other = lax.ppermute(gathered, AXES, [(i, i ^ 2) for i in range(devices)])
-    slots = devices // 2
-
-    place_arr = place.reshape(1)
+
     new_rows = pl.pallas_call(
         functools.partial(tracer_kernel, count, blocks),
-        out_shape=tile_shape(2 * count * SUB),
-        in_specs=[SMEM_SPEC, SMEM_SPEC] + [VMEM_SPEC] * 6,
+        out_shape=tile_shape(rows),
+        in_specs=[SMEM_SPEC] + [VMEM_SPEC] * 6,
         out_specs=VMEM_SPEC,
+        compiler_params=SMALL_GRANT,
         name="tracer",
-    )(place_arr, vdiff, tracer_rows, velocity_rows, depth_levels, near, far, edge_pack)
-
+    )(vdiff, tracer_rows, velocity_rows, depth, near, far, edges)
+
+    slots = devices // 2
     surface, residual = pl.pallas_call(
         functools.partial(solve_kernel, count, blocks, tuple(order)),
         out_shape=[tile_shape(SUB), tile_shape(SUB)],
-        in_specs=[SMEM_SPEC] + [VMEM_SPEC] * 2,
+        in_specs=[VMEM_SPEC] * 2,
         out_specs=[VMEM_SPEC] * 2,
-        scratch_shapes=[
-            pltpu.VMEM((3, 2, blocks * SUB, LANE), jnp.float32),
-            pltpu.VMEM((2, blocks * SUB, LANE), jnp.float32),
-        ],
+        scratch_shapes=[pltpu.VMEM((2, blocks * SUB, LANE), jnp.float32)],
+        compiler_params=SMALL_GRANT,
         name="solve",
-    )(place_arr, gathered.reshape(slots, 3 * SUB, LANE), other.reshape(slots, 3 * SUB, LANE))
+    )(gathered.reshape(slots, 3 * SUB, LANE), other.reshape(slots, 3 * SUB, LANE))
     return new_rows.reshape(tracers.shape), surface, residual
 
 

time: 34.6 us -> 27.1 us (0.78)
  starting transfers between devices: 14.3 us -> 7.78 us
  waiting for transfers between devices: 10.1 us -> 13.3 us
  Pallas kernels: 6.46 us -> 4.34 us
  local copies, waits for them, and re-layouts: 2.66 us -> 0.68 us
    ppermute x1, starting transfers between devices: 5.35 us -> 0.45 us  [small_shards(): other = lax.ppermute(gathered, AXES, [(i, i ^ 2) for i in range(devices)])]
    ppermute x6, waiting for transfers between devices: 10.1 us -> 13.3 us  [the longest x3 7.88 us: small_shards(): came = lax.ppermute(gathered, AXES, pairs)]
    unnamed x21 -> x5, local copies, waits for them, and re-layouts: 2.64 us -> 0.66 us
    ppermute x6, starting transfers between devices: 8.98 us -> 7.32 us  [the longest x3 4.58 us: small_shards(): came = lax.ppermute(gathered, AXES, pairs)]
    pallas_call x1, Pallas kernels: 2.75 us -> 1.64 us  [small_shards(): pl.pallas_call(functools.partial(solve_kernel, count, blocks, tuple(order...]
    pallas_call x1, Pallas kernels: 1.74 us -> 1.19 us  [small_shards(): pl.pallas_call(functools.partial(pack_kernel, count), out_shape=[tile_sha...]
    pallas_call x1, Pallas kernels: 1.97 us -> 1.52 us  [small_shards(): pl.pallas_call(functools.partial(tracer_kernel, count, blocks), out_shape...]
  transfers between devices with their start and end apart: 7 -> 7, of which waited for: 5 -> 5; matrix products, arithmetic and copies ran while one was open for 2% -> 0% of each run, Pallas kernels for 6% -> 6%
where the time goes in v2:
time: 27.1 us; the launch traced here: 26.7 us
  waiting for transfers between devices  13.3 us (49%)
  starting transfers between devices  7.78 us (29%)
  Pallas kernels  4.34 us (16%)
  local copies, waits for them, and re-layouts  0.68 us (3%)
  between operations  0.67 us (2%)
    ppermute x3, waiting for transfers between devices, small_shards(): came = lax.ppermute(gathered, AXES, pairs)  7.88 us
    ppermute x3, starting transfers between devices, small_shards(): came = lax.ppermute(gathered, AXES, pairs)  4.58 us
    ppermute x1, waiting for transfers between devices, small_shards(): far = lax.ppermute(far, AXES, far_pairs + [(0, 1), (1, 0)])  2.95 us
    ppermute x1, waiting for transfers between devices, small_shards(): lax.ppermute(jnp.concatenate([gathered, near[halo_rows:]], 0), AXES, pairs)  2.43 us
    pallas_call x1, Pallas kernels, small_shards(): pl.pallas_call(functools.partial(solve_kernel, count, blocks, tuple(order...  1.64 us
    pallas_call x1, Pallas kernels, small_shards(): pl.pallas_call(functools.partial(tracer_kernel, count, blocks), out_shape...  1.52 us
    ppermute x1, starting transfers between devices, small_shards(): lax.ppermute(jnp.concatenate([gathered, near[halo_rows:]], 0), AXES, pairs)  1.49 us
    ppermute x1, starting transfers between devices, small_shards(): far = lax.ppermute(far, AXES, far_pairs + [(0, 1), (1, 0)])  1.25 us
  transfers between devices with their start and end apart: 7, of which 5 were waited for; matrix products, arithmetic and copies ran while one was open for 0% of the time, Pallas kernels for 6%

profile of v2, /device:TPU:5, one launch (start us, length us, event | category | flops | bytes accessed | tf_op | source)
XLA Modules:
  0.0 26.7 jit_solution(10097945077396337932)
XLA Ops:
  0.6 1.2 %pack.1 = (f32[24,128]{1,0:T(8,128)S(1)}, f32[72,128]{1,0:T(8,128)S(1)}, f32[56,128]{1,0:T(8,128)S(1)}, f32[256,128]{1,0:T(8,128)S(1)}, f32[256,128]{1,0:T(8,128)S(1)}, /*index=5*/s32[8,128]{1,0:T(8,128)S(1)}) custom-call(f32[256,128]{1,0:T(8,128)} %bitcast.8, f32[256,128]{1,0:T(8,128)} %bitcast.9, s32[8,128]{1,0:T(8,128)} %depth_hbm.1), custom_call_target="tpu_custom_call" | custom-call | tf_op jit(solution)/shard_map/pack/pallas_call | solution.py:445
  1.8 2.9 %collective-permute-start.2 = (f32[24,128]{1,0:T(8,128)S(1)}, f32[24,128]{1,0:T(8,128)S(1)}, u32[]{:S(2)}, u32[]{:S(2)}) collective-permute-start(f32[24,128]{1,0:T(8,128)S(1)} %get-tuple-element.16), channel_id=1, source_target_pairs={{0,18},{1,19},{2,16},{3,17},{4,22},{5,23},{6,20},{7,21},{8,26},{9,... | collective-permute-start | bytes 36872 | tf_op jit(solution)/shard_map/ppermute | solution.py:478
  4.8 0.0 collective-permute-start
  4.8 1.4 %collective-permute-done.2 = f32[24,128]{1,0:T(8,128)S(1)} collective-permute-done((f32[24,128]{1,0:T(8,128)S(1)}, f32[24,128]{1,0:T(8,128)S(1)}, u32[]{:S(2)}, u32[]{:S(2)}) %collective-permute-start.2) | collective-permute-done | bytes 12320 | tf_op jit(solution)/shard_map/ppermute | solution.py:478
  6.2 1.6 %collective-permute-start.3 = (f32[48,128]{1,0:T(8,128)S(1)}, f32[48,128]{1,0:T(8,128)S(1)}, u32[]{:S(2)}, u32[]{:S(2)}) collective-permute-start(f32[48,128]{1,0:T(8,128)S(1)} %pad_maximum_fusion.2), channel_id=1, source_target_pairs={{0,10},{1,11},{2,8},{3,9},{4,14},{5,15},{6,12},{7,13},{8,2},{9,3},... | collective-permute-start | bytes 73736 | tf_op jit(solution)/shard_map/ppermute | solution.py:478
  7.8 0.0 collective-permute-done.near_ref
  7.8 1.7 %collective-permute-done.3 = f32[48,128]{1,0:T(8,128)S(1)} collective-permute-done((f32[48,128]{1,0:T(8,128)S(1)}, f32[48,128]{1,0:T(8,128)S(1)}, u32[]{:S(2)}, u32[]{:S(2)}) %collective-permute-start.3) | collective-permute-done | bytes 24608 | tf_op jit(solution)/shard_map/ppermute | solution.py:478
  9.5 1.5 %collective-permute-start.4 = (f32[112,128]{1,0:T(8,128)S(1)}, f32[112,128]{1,0:T(8,128)S(1)}, u32[]{:S(2)}, u32[]{:S(2)}) collective-permute-start(f32[112,128]{1,0:T(8,128)S(1)} %pad_maximum_fusion.1), channel_id=1, source_target_pairs={{0,3},{1,2},{2,1},{3,0},{4,7},{5,6},{6,5},{7,4},{8,11},{9,10},{10,... | collective-permute-start | bytes 172040 | tf_op jit(solution)/shard_map/ppermute | solution.py:475
  10.9 2.4 %collective-permute-done.4.edge_ref = f32[112,128]{1,0:T(8,128)S(1)} collective-permute-done((f32[112,128]{1,0:T(8,128)S(1)}, f32[112,128]{1,0:T(8,128)S(1)}, u32[]{:S(2)}, u32[]{:S(2)}) %collective-permute-start.4) | collective-permute-done | bytes 57376 | tf_op jit(solution)/shard_map/ppermute | solution.py:475
  13.4 0.1 collective-permute-start.5
  13.5 4.8 %collective-permute-done.5 = f32[192,128]{1,0:T(8,128)S(1)} collective-permute-done((f32[192,128]{1,0:T(8,128)S(1)}, f32[192,128]{1,0:T(8,128)S(1)}, u32[]{:S(2)}, u32[]{:S(2)}) %collective-permute-start.5) | collective-permute-done | bytes 98336 | tf_op jit(solution)/shard_map/ppermute | solution.py:478
  18.3 0.5 %collective-permute-start.6 = (f32[384,128]{1,0:T(8,128)S(1)}, f32[384,128]{1,0:T(8,128)S(1)}, u32[]{:S(2)}, u32[]{:S(2)}) collective-permute-start(f32[384,128]{1,0:T(8,128)S(1)} %constant_dynamic-update-slice_fusion), channel_id=1, source_target_pairs={{0,2},{1,3},{2,0},{3,1},{4,6},{5,7},{6,4},{7,5},{8,10},{9,11},{10,... | collective-permute-start | bytes 589832 | tf_op jit(solution)/shard_map/ppermute | solution.py:480
  18.7 1.2 %collective-permute-start.1 = (f32[56,128]{1,0:T(8,128)S(1)}, f32[56,128]{1,0:T(8,128)S(1)}, u32[]{:S(2)}, u32[]{:S(2)}) collective-permute-start(f32[56,128]{1,0:T(8,128)S(1)} %get-tuple-element.15), channel_id=1, source_target_pairs={{2,4},{4,2},{3,5},{5,3},{6,8},{8,6},{7,9},{9,7},{10,12},{12,10},{1... | collective-permute-start | bytes 86024 | tf_op jit(solution)/shard_map/ppermute | solution.py:468
  20.0 2.9 %collective-permute-done.1.far_ref = f32[56,128]{1,0:T(8,128)S(1)} collective-permute-done((f32[56,128]{1,0:T(8,128)S(1)}, f32[56,128]{1,0:T(8,128)S(1)}, u32[]{:S(2)}, u32[]{:S(2)}) %collective-permute-start.1) | collective-permute-done | bytes 28704 | tf_op jit(solution)/shard_map/ppermute | solution.py:468
  22.9 0.0 copy-start
  22.9 0.7 %copy-done = f32[15]{0:T(128)S(1)} copy-done((f32[15]{0:T(128)S(1)}, f32[15]{0:T(128)}, u32[]{:S(2)}) %copy-start) | copy-done | bytes 84
  23.6 1.5 %tracer.1 = f32[256,128]{1,0:T(8,128)} custom-call(f32[15]{0:T(128)S(1)} %copy-done, f32[256,128]{1,0:T(8,128)S(1)} %get-tuple-element.11.tracers_ref, f32[256,128]{1,0:T(8,128)S(1)} %get-tuple-element.12.velocity_ref, s32[8,128]{1,0:T(8,128)S(1)} %get-tuple-element.13.depth_ref, f32[72,128]{1,0:T(8,128)S(1)} %collective-permute-done.near_ref, ...), custom_call_target="tpu_custom_call" | custom-call | tf_op jit(solution)/shard_map/tracer/pallas_call | solution.py:482
  25.1 0.0 collective-permute-done.6
  25.1 1.6 %solve.1 = (f32[8,128]{1,0:T(8,128)}, f32[8,128]{1,0:T(8,128)}) custom-call(f32[16,24,128]{2,1,0:T(8,128)S(1)} %bitcast.5, f32[16,24,128]{2,1,0:T(8,128)S(1)} %bitcast.6), custom_call_target="tpu_custom_call" | custom-call | tf_op jit(solution)/shard_map/solve/pallas_call | solution.py:492
  (9 shorter events, 0.0 us)
Async XLA Ops:
  1.8 4.4 %collective-permute-start.2 = (f32[24,128]{1,0:T(8,128)S(1)}, f32[24,128]{1,0:T(8,128)S(1)}, u32[]{:S(2)}, u32[]{:S(2)}) collective-permute-start(f32[24,128]{1,0:T(8,128)S(1)} %get-tuple-element.16), channel_id=1, source_target_pairs={{0,18},{1,19},{2,16},{3,17},{4,22},{5,23},{6,20},{7,21},{8,26},{9,... | collective-permute-start | bytes 36872 | tf_op jit(solution)/shard_map/ppermute | solution.py:478
  4.8 3.0 %collective-permute-start = (f32[72,128]{1,0:T(8,128)S(1)}, f32[72,128]{1,0:T(8,128)S(1)}, u32[]{:S(2)}, u32[]{:S(2)}) collective-permute-start(f32[72,128]{1,0:T(8,128)S(1)} %get-tuple-element.14), channel_id=1, source_target_pairs={{0,2},{1,3},{2,0},{3,1},{4,6},{5,7},{6,4},{7,5},{8,10},{9,11},{10,... | collective-permute-start | bytes 110600 | tf_op jit(solution)/shard_map/ppermute | solution.py:462
  6.2 3.3 %collective-permute-start.3 = (f32[48,128]{1,0:T(8,128)S(1)}, f32[48,128]{1,0:T(8,128)S(1)}, u32[]{:S(2)}, u32[]{:S(2)}) collective-permute-start(f32[48,128]{1,0:T(8,128)S(1)} %pad_maximum_fusion.2), channel_id=1, source_target_pairs={{0,10},{1,11},{2,8},{3,9},{4,14},{5,15},{6,12},{7,13},{8,2},{9,3},... | collective-permute-start | bytes 73736 | tf_op jit(solution)/shard_map/ppermute | solution.py:478
  9.5 3.9 %collective-permute-start.4 = (f32[112,128]{1,0:T(8,128)S(1)}, f32[112,128]{1,0:T(8,128)S(1)}, u32[]{:S(2)}, u32[]{:S(2)}) collective-permute-start(f32[112,128]{1,0:T(8,128)S(1)} %pad_maximum_fusion.1), channel_id=1, source_target_pairs={{0,3},{1,2},{2,1},{3,0},{4,7},{5,6},{6,5},{7,4},{8,11},{9,10},{10,... | collective-permute-start | bytes 172040 | tf_op jit(solution)/shard_map/ppermute | solution.py:475
  13.4 4.9 %collective-permute-start.5 = (f32[192,128]{1,0:T(8,128)S(1)}, f32[192,128]{1,0:T(8,128)S(1)}, u32[]{:S(2)}, u32[]{:S(2)}) collective-permute-start(f32[192,128]{1,0:T(8,128)S(1)} %pad_maximum_fusion), channel_id=1, source_target_pairs={{0,6},{1,7},{2,4},{3,5},{4,2},{5,3},{6,0},{7,1},{8,14},{9,15},{10,... | collective-permute-start | bytes 294920 | tf_op jit(solution)/shard_map/ppermute | solution.py:478
  18.3 6.8 %collective-permute-start.6 = (f32[384,128]{1,0:T(8,128)S(1)}, f32[384,128]{1,0:T(8,128)S(1)}, u32[]{:S(2)}, u32[]{:S(2)}) collective-permute-start(f32[384,128]{1,0:T(8,128)S(1)} %constant_dynamic-update-slice_fusion), channel_id=1, source_target_pairs={{0,2},{1,3},{2,0},{3,1},{4,6},{5,7},{6,4},{7,5},{8,10},{9,11},{10,... | collective-permute-start | bytes 589832 | tf_op jit(solution)/shard_map/ppermute | solution.py:480
  18.7 4.2 %collective-permute-start.1 = (f32[56,128]{1,0:T(8,128)S(1)}, f32[56,128]{1,0:T(8,128)S(1)}, u32[]{:S(2)}, u32[]{:S(2)}) collective-permute-start(f32[56,128]{1,0:T(8,128)S(1)} %get-tuple-element.15), channel_id=1, source_target_pairs={{2,4},{4,2},{3,5},{5,3},{6,8},{8,6},{7,9},{9,7},{10,12},{12,10},{1... | collective-permute-start | bytes 86024 | tf_op jit(solution)/shard_map/ppermute | solution.py:468
  22.9 0.7 %copy-start = (f32[15]{0:T(128)S(1)}, f32[15]{0:T(128)}, u32[]{:S(2)}) copy-start(f32[15]{0:T(128)} %vdiff_ref.1) | copy-start | bytes 184

commit v3 on v2

--- a/solution.py
+++ b/solution.py
@@ -186,9 +186,7 @@
     return jnp.take_along_axis(value, index, axis=1)
 
 
-def pack_kernel(
-    count, tracers_hbm, velocity_hbm, depth_hbm, sums_ref, near_ref, far_ref, tracers_ref, velocity_ref, depth_ref, sems
-):
+def sums_kernel(count, tracers_hbm, velocity_hbm, depth_hbm, sums_ref, tracers_ref, velocity_ref, depth_ref, sems):
     copies = [
         pltpu.make_async_copy(src, dst, sems.at[at])
         for at, (src, dst) in enumerate(
@@ -197,7 +195,6 @@
     ]
     for copy in copies:
         copy.start()
-    odd = lax.axis_index("blk") % 2 == 1
     copies[0].wait()
     copies[1].wait()
     depth = depth_ref[...]
@@ -207,19 +204,23 @@
         wet = depth > level
         east += jnp.where(wet, velocity_ref[pl.ds(level * SUB, SUB), :], 0.0)
         north += jnp.where(wet, velocity_ref[pl.ds((count + level) * SUB, SUB), :], 0.0)
-    depth_f = depth.astype(jnp.float32)
     sums_ref[0:SUB, :] = east
     sums_ref[SUB : 2 * SUB, :] = north
-    sums_ref[2 * SUB : 3 * SUB, :] = depth_f
+    sums_ref[2 * SUB : 3 * SUB, :] = depth.astype(jnp.float32)
     copies[2].wait()
+
+
+def pack_kernel(count, tracers_ref, velocity_ref, depth_ref, near_ref, far_ref):
+    odd = lax.axis_index("blk") % 2 == 1
+    depth = depth_ref[...].astype(jnp.float32)
 
     def both(ref, first, rows):
         low = ref[pl.ds(first, rows, stride=SUB), :]
         high = ref[pl.ds(first + SUB - 1, rows, stride=SUB), :]
         return jnp.where(odd, low, high), jnp.where(odd, high, low)
 
-    depth_low = jnp.broadcast_to(depth_f[0:1, :], (SUB, LANE))
-    depth_high = jnp.broadcast_to(depth_f[SUB - 1 : SUB, :], (SUB, LANE))
+    depth_low = jnp.broadcast_to(depth[0:1, :], (SUB, LANE))
+    depth_high = jnp.broadcast_to(depth[SUB - 1 : SUB, :], (SUB, LANE))
     parts = (
         both(tracers_ref, 0, 2 * count),
         both(velocity_ref, count * SUB, count),
@@ -239,7 +240,7 @@
         elif field < 3 * count:
             tile = velocity_ref[pl.ds((field - 2 * count) * SUB, SUB), :]
         else:
-            tile = depth_f
+            tile = depth
         west_pack = jnp.where(lane == field, pltpu.roll(tile, field, 1), west_pack)
         east_pack = jnp.where(lane == field, pltpu.roll(tile, field + 1, 1), east_pack)
     near_ref[at : at + SUB, :] = west_pack
@@ -321,25 +322,23 @@
             out_ref[pl.ds(field * SUB, SUB), :] = jnp.where(depth > k, here + TIME_STEP * tendency, 0.0)
 
 
-def solve_kernel(count, blocks, order, own_ref, other_ref, surface_ref, residual_ref, scratch):
+def solve_kernel(
+    count, blocks, apart, own_ref, other_ref, rows_ref, surface_ref, residual_ref, rows_hbm, fields, scratch, sem
+):
+    leaving = pltpu.make_async_copy(rows_ref, rows_hbm, sem)
+    leaving.start()
     me = lax.axis_index("blk") * 2 + lax.axis_index("grp")
     height = blocks * SUB
 
-    def slot_of(place):
-        return sum(((place >> at) & 1) << bit for bit, at in enumerate(order))
-
-    def core_of(place):
-        return sum((place >> at) & 1 for at in (*order, 1)) & 1
-
-    my_slot, my_core = slot_of(me), core_of(me)
-
-    def tile(part, place):
+    for slot, mask in enumerate(apart):
+        fields[me ^ mask] = own_ref[slot]
+        fields[me ^ (mask ^ 2)] = other_ref[slot]
+
+    def field(part):
         rows = slice(part * SUB, (part + 1) * SUB)
-        slot = slot_of(place) ^ my_slot
-        return jnp.where(my_core == core_of(place), own_ref[slot, rows, :], other_ref[slot, rows, :])
-
-    def field(part):
-        return tuple(jnp.concatenate([tile(part, blk * 2 + grp) for blk in range(blocks)], 0) for grp in range(2))
+        return tuple(
+            jnp.concatenate([fields[blk * 2 + grp, rows, :] for blk in range(blocks)], 0) for grp in range(2)
+        )
 
     shape = (height, LANE)
     lane = lax.broadcasted_iota(jnp.int32, shape, 1)
@@ -424,6 +423,7 @@
             norm_now = norm_next
     surface_ref[...] = own_surface
     residual_ref[...] = own_residual
+    leaving.wait()
 
 
 VMEM_SPEC = pl.BlockSpec(memory_space=pltpu.VMEM)
@@ -433,6 +433,11 @@
 
 def tile_shape(rows):
     return jax.ShapeDtypeStruct((rows, LANE), jnp.float32)
+
+
+def gather_stages(devices):
+    single = [(1 << bit | 2,) for bit in range(devices.bit_length() - 2, 2, -1)]
+    return [*single, (7, 3, 6)]
 
 
 def small_shards(tracers, velocity, depth_levels, vdiff):
@@ -442,22 +447,29 @@
     rows = 2 * count * SUB
     halo_rows = 3 * count + SUB
 
-    sums, near, far, tracer_rows, velocity_rows, depth = pl.pallas_call(
-        functools.partial(pack_kernel, count),
+    arguments = (tracers.reshape(rows, LANE), velocity.reshape(rows, LANE), depth_levels)
+    sums, tracer_rows, velocity_rows, depth = pl.pallas_call(
+        functools.partial(sums_kernel, count),
         out_shape=[
             tile_shape(3 * SUB),
-            tile_shape(halo_rows + 2 * SUB),
-            tile_shape(halo_rows),
             tile_shape(rows),
             tile_shape(rows),
             jax.ShapeDtypeStruct((SUB, LANE), jnp.int32),
         ],
         in_specs=[pl.BlockSpec(memory_space=pltpu.HBM)] * 3,
-        out_specs=[VMEM_SPEC] * 6,
+        out_specs=[VMEM_SPEC] * 4,
         scratch_shapes=[pltpu.SemaphoreType.DMA((3,))],
         compiler_params=SMALL_GRANT,
+        name="sums",
+    )(*(pltpu.with_memory_space_constraint(x, pltpu.HBM) for x in arguments))
+    near, far = pl.pallas_call(
+        functools.partial(pack_kernel, count),
+        out_shape=[tile_shape(halo_rows + 2 * SUB), tile_shape(halo_rows)],
+        in_specs=[VMEM_SPEC] * 3,
+        out_specs=[VMEM_SPEC] * 2,
+        compiler_params=SMALL_GRANT,
         name="pack",
-    )(*(pltpu.with_memory_space_constraint(x, pltpu.HBM) for x in (tracers.reshape(rows, LANE), velocity.reshape(rows, LANE), depth_levels)))
+    )(tracer_rows, velocity_rows, depth)
 
     near = lax.ppermute(near, AXES, [(i, i ^ 2) for i in range(devices)])
     far_pairs = []
@@ -467,21 +479,23 @@
             far_pairs += [(here, here ^ 1)] if blk == blocks - 1 else [(here, here + 2), (here + 2, here)]
     far = lax.ppermute(far, AXES, far_pairs + [(0, 1), (1, 0)])
 
-    order = [*range(devices.bit_length() - 2, 2, -1), 0, 2]
-    gathered, edges = sums, None
-    for bit in order:
-        pairs = [(i, i ^ (1 << bit | 2)) for i in range(devices)]
-        if bit == 0:
-            edges = lax.ppermute(jnp.concatenate([gathered, near[halo_rows:]], 0), AXES, pairs)
-            came = edges[: gathered.shape[0]]
-        else:
-            came = lax.ppermute(gathered, AXES, pairs)
-        gathered = jnp.concatenate([gathered, came], 0)
+    gathered, edges, apart = sums, None, [0]
+    for masks in gather_stages(devices):
+        pieces = [gathered]
+        for mask in masks:
+            pairs = [(i, i ^ mask) for i in range(devices)]
+            if mask & 1:
+                edges = lax.ppermute(jnp.concatenate([gathered, near[halo_rows:]], 0), AXES, pairs)
+                pieces.append(edges[: gathered.shape[0]])
+            else:
+                pieces.append(lax.ppermute(gathered, AXES, pairs))
+        gathered = jnp.concatenate(pieces, 0)
+        apart = apart + [came ^ mask for mask in masks for came in apart]
     other = lax.ppermute(gathered, AXES, [(i, i ^ 2) for i in range(devices)])
 
     new_rows = pl.pallas_call(
         functools.partial(tracer_kernel, count, blocks),
-        out_shape=tile_shape(rows),
+        out_shape=pltpu.VMEM((rows, LANE), jnp.float32),
         in_specs=[SMEM_SPEC] + [VMEM_SPEC] * 6,
         out_specs=VMEM_SPEC,
         compiler_params=SMALL_GRANT,
@@ -489,15 +503,19 @@
     )(vdiff, tracer_rows, velocity_rows, depth, near, far, edges)
 
     slots = devices // 2
-    surface, residual = pl.pallas_call(
-        functools.partial(solve_kernel, count, blocks, tuple(order)),
-        out_shape=[tile_shape(SUB), tile_shape(SUB)],
-        in_specs=[VMEM_SPEC] * 2,
-        out_specs=[VMEM_SPEC] * 2,
-        scratch_shapes=[pltpu.VMEM((2, blocks * SUB, LANE), jnp.float32)],
+    surface, residual, new_rows = pl.pallas_call(
+        functools.partial(solve_kernel, count, blocks, tuple(apart)),
+        out_shape=[tile_shape(SUB), tile_shape(SUB), tile_shape(rows)],
+        in_specs=[VMEM_SPEC] * 3,
+        out_specs=[VMEM_SPEC, VMEM_SPEC, pl.BlockSpec(memory_space=pltpu.HBM)],
+        scratch_shapes=[
+            pltpu.VMEM((devices, 3 * SUB, LANE), jnp.float32),
+            pltpu.VMEM((2, blocks * SUB, LANE), jnp.float32),
+            pltpu.SemaphoreType.DMA,
+        ],
         compiler_params=SMALL_GRANT,
         name="solve",
-    )(gathered.reshape(slots, 3 * SUB, LANE), other.reshape(slots, 3 * SUB, LANE))
+    )(gathered.reshape(slots, 3 * SUB, LANE), other.reshape(slots, 3 * SUB, LANE), new_rows)
     return new_rows.reshape(tracers.shape), surface, residual
 
 

time: 27.1 us -> 24.7 us (0.911)
  the two profiles are of different devices: /device:TPU:5 before, /device:TPU:0 now
where the time goes in v3:
time: 24.7 us; the launch traced here: 24.5 us
  starting transfers between devices  11.2 us (45%)
  waiting for transfers between devices  8.91 us (36%)
  Pallas kernels  3.73 us (15%)
  between operations  0.68 us (3%)
    ppermute x3, starting transfers between devices, small_shards(): pieces.append(lax.ppermute(gathered, AXES, pairs))  5.63 us
    ppermute x3, waiting for transfers between devices, small_shards(): pieces.append(lax.ppermute(gathered, AXES, pairs))  3.5 us
    ppermute x2, starting transfers between devices, small_shards(): lax.ppermute(jnp.concatenate([gathered, near[halo_rows:]], 0), AXES, pairs)  3.14 us
    ppermute x2, waiting for transfers between devices, small_shards(): lax.ppermute(jnp.concatenate([gathered, near[halo_rows:]], 0), AXES, pairs)  3.03 us
    ppermute x1, waiting for transfers between devices, small_shards(): far = lax.ppermute(far, AXES, far_pairs + [(0, 1), (1, 0)])  2.38 us
    pallas_call x1, Pallas kernels, small_shards(): pl.pallas_call(functools.partial(solve_kernel, count, blocks, tuple(apart...  1.7 us
    ppermute x1, starting transfers between devices, small_shards(): far = lax.ppermute(far, AXES, far_pairs + [(0, 1), (1, 0)])  1.49 us
    pallas_call x1, Pallas kernels, small_shards(): pl.pallas_call(functools.partial(sums_kernel, count), out_shape=[tile_sha...  1.01 us
  transfers between devices with their start and end apart: 8, of which 5 were waited for; matrix products, arithmetic and copies ran while one was open for 0% of the time, Pallas kernels for 4%

profile of v3, /device:TPU:0, one launch (start us, length us, event | category | flops | bytes accessed | tf_op | source)
XLA Modules:
  0.0 24.5 jit_solution(9730860628767336879)
XLA Ops:
  0.6 1.0 %sums.1 = (f32[24,128]{1,0:T(8,128)S(1)}, f32[256,128]{1,0:T(8,128)S(1)}, f32[256,128]{1,0:T(8,128)S(1)}, s32[8,128]{1,0:T(8,128)S(1)}) custom-call(f32[256,128]{1,0:T(8,128)} %bitcast.7, f32[256,128]{1,0:T(8,128)} %bitcast.8, s32[8,128]{1,0:T(8,128)} %depth_hbm.1), custom_call_target="tpu_custom_call" | custom-call | tf_op jit(solution)/shard_map/sums/pallas_call | solution.py:451
  1.6 3.6 %collective-permute-start = (f32[24,128]{1,0:T(8,128)S(1)}, f32[24,128]{1,0:T(8,128)S(1)}, u32[]{:S(2)}, u32[]{:S(2)}) collective-permute-start(f32[24,128]{1,0:T(8,128)S(1)} %get-tuple-element.12), channel_id=1, source_target_pairs={{0,18},{1,19},{2,16},{3,17},{4,22},{5,23},{6,20},{7,21},{8,26},{9,... | collective-permute-start | bytes 36872 | tf_op jit(solution)/shard_map/ppermute | solution.py:491
  5.2 0.2 pack.1
  5.4 0.7 %collective-permute-start.2 = (f32[72,128]{1,0:T(8,128)S(1)}, f32[72,128]{1,0:T(8,128)S(1)}, u32[]{:S(2)}, u32[]{:S(2)}) collective-permute-start(f32[72,128]{1,0:T(8,128)S(1)} %get-tuple-element.16), channel_id=1, source_target_pairs={{0,2},{1,3},{2,0},{3,1},{4,6},{5,7},{6,4},{7,5},{8,10},{9,11},{10,... | collective-permute-start | bytes 110600 | tf_op jit(solution)/shard_map/ppermute | solution.py:474
  6.1 0.5 %collective-permute-done = f32[24,128]{1,0:T(8,128)S(1)} collective-permute-done((f32[24,128]{1,0:T(8,128)S(1)}, f32[24,128]{1,0:T(8,128)S(1)}, u32[]{:S(2)}, u32[]{:S(2)}) %collective-permute-start) | collective-permute-done | bytes 12320 | tf_op jit(solution)/shard_map/ppermute | solution.py:491
  6.6 1.9 %collective-permute-start.1 = (f32[48,128]{1,0:T(8,128)S(1)}, f32[48,128]{1,0:T(8,128)S(1)}, u32[]{:S(2)}, u32[]{:S(2)}) collective-permute-start(f32[48,128]{1,0:T(8,128)S(1)} %pad_maximum_fusion.2), channel_id=1, source_target_pairs={{0,10},{1,11},{2,8},{3,9},{4,14},{5,15},{6,12},{7,13},{8,2},{9,3},... | collective-permute-start | bytes 73736 | tf_op jit(solution)/shard_map/ppermute | solution.py:491
  8.5 0.0 collective-permute-done.2.near_ref
  8.5 1.5 %collective-permute-done.1 = f32[48,128]{1,0:T(8,128)S(1)} collective-permute-done((f32[48,128]{1,0:T(8,128)S(1)}, f32[48,128]{1,0:T(8,128)S(1)}, u32[]{:S(2)}, u32[]{:S(2)}) %collective-permute-start.1) | collective-permute-done | bytes 24608 | tf_op jit(solution)/shard_map/ppermute | solution.py:491
  10.0 1.6 %collective-permute-start.4 = (f32[112,128]{1,0:T(8,128)S(1)}, f32[112,128]{1,0:T(8,128)S(1)}, u32[]{:S(2)}, u32[]{:S(2)}) collective-permute-start(f32[112,128]{1,0:T(8,128)S(1)} %pad_maximum_fusion), channel_id=1, source_target_pairs={{0,3},{1,2},{2,1},{3,0},{4,7},{5,6},{6,5},{7,4},{8,11},{9,10},{10,... | collective-permute-start | bytes 172040 | tf_op jit(solution)/shard_map/ppermute | solution.py:488
  11.7 1.5 %collective-permute-start.3 = (f32[112,128]{1,0:T(8,128)S(1)}, f32[112,128]{1,0:T(8,128)S(1)}, u32[]{:S(2)}, u32[]{:S(2)}) collective-permute-start(f32[112,128]{1,0:T(8,128)S(1)} %pad_maximum_fusion), channel_id=1, source_target_pairs={{0,7},{1,6},{2,5},{3,4},{4,3},{5,2},{6,1},{7,0},{8,15},{9,14},{10,... | collective-permute-start | bytes 172040 | tf_op jit(solution)/shard_map/ppermute | solution.py:488
  13.2 0.2 collective-permute-start.5
  13.4 3.0 %collective-permute-done.3 = f32[112,128]{1,0:T(8,128)S(1)} collective-permute-done((f32[112,128]{1,0:T(8,128)S(1)}, f32[112,128]{1,0:T(8,128)S(1)}, u32[]{:S(2)}, u32[]{:S(2)}) %collective-permute-start.3) | collective-permute-done | bytes 57376 | tf_op jit(solution)/shard_map/ppermute | solution.py:488
  16.4 0.0 collective-permute-done.4.edge_ref
  16.4 1.5 %collective-permute-done.5 = f32[96,128]{1,0:T(8,128)S(1)} collective-permute-done((f32[96,128]{1,0:T(8,128)S(1)}, f32[96,128]{1,0:T(8,128)S(1)}, u32[]{:S(2)}, u32[]{:S(2)}) %collective-permute-start.5) | collective-permute-done | bytes 49184 | tf_op jit(solution)/shard_map/ppermute | solution.py:491
  17.9 0.0 copy-start
  17.9 0.2 collective-permute-start.6
  18.1 1.5 %collective-permute-start.7 = (f32[56,128]{1,0:T(8,128)S(1)}, f32[56,128]{1,0:T(8,128)S(1)}, u32[]{:S(2)}, u32[]{:S(2)}) collective-permute-start(f32[56,128]{1,0:T(8,128)S(1)} %get-tuple-element.17), channel_id=1, source_target_pairs={{2,4},{4,2},{3,5},{5,3},{6,8},{8,6},{7,9},{9,7},{10,12},{12,10},{1... | collective-permute-start | bytes 86024 | tf_op jit(solution)/shard_map/ppermute | solution.py:480
  19.6 2.4 %collective-permute-done.7.far_ref = f32[56,128]{1,0:T(8,128)S(1)} collective-permute-done((f32[56,128]{1,0:T(8,128)S(1)}, f32[56,128]{1,0:T(8,128)S(1)}, u32[]{:S(2)}, u32[]{:S(2)}) %collective-permute-start.7) | collective-permute-done | bytes 28704 | tf_op jit(solution)/shard_map/ppermute | solution.py:480
  22.0 0.0 copy-done
  22.0 0.9 %tracer.1.rows_ref = f32[256,128]{1,0:T(8,128)S(1)} custom-call(f32[15]{0:T(128)S(1)} %copy-done, f32[256,128]{1,0:T(8,128)S(1)} %get-tuple-element.13.tracers_ref, f32[256,128]{1,0:T(8,128)S(1)} %get-tuple-element.14.velocity_ref, s32[8,128]{1,0:T(8,128)S(1)} %get-tuple-element.15.depth_ref, f32[72,128]{1,0:T(8,128)S(1)} %collective-permute-done.2.near_ref, ...), custom_call_target="tpu_custom_call" | custom-call | tf_op jit(solution)/shard_map/tracer/pallas_call | solution.py:496
  22.8 0.0 collective-permute-done.6
  22.8 1.7 %solve.1 = (f32[8,128]{1,0:T(8,128)}, f32[8,128]{1,0:T(8,128)}, f32[256,128]{1,0:T(8,128)}) custom-call(f32[16,24,128]{2,1,0:T(8,128)S(1)} %bitcast.5, f32[16,24,128]{2,1,0:T(8,128)S(1)} %bitcast.6, f32[256,128]{1,0:T(8,128)S(1)} %tracer.1.rows_ref), custom_call_target="tpu_custom_call" | custom-call | tf_op jit(solution)/shard_map/solve/pallas_call | solution.py:506
  (10 shorter events, 0.0 us)
Async XLA Ops:
  1.6 5.0 %collective-permute-start = (f32[24,128]{1,0:T(8,128)S(1)}, f32[24,128]{1,0:T(8,128)S(1)}, u32[]{:S(2)}, u32[]{:S(2)}) collective-permute-start(f32[24,128]{1,0:T(8,128)S(1)} %get-tuple-element.12), channel_id=1, source_target_pairs={{0,18},{1,19},{2,16},{3,17},{4,22},{5,23},{6,20},{7,21},{8,26},{9,... | collective-permute-start | bytes 36872 | tf_op jit(solution)/shard_map/ppermute | solution.py:491
  5.4 3.1 %collective-permute-start.2 = (f32[72,128]{1,0:T(8,128)S(1)}, f32[72,128]{1,0:T(8,128)S(1)}, u32[]{:S(2)}, u32[]{:S(2)}) collective-permute-start(f32[72,128]{1,0:T(8,128)S(1)} %get-tuple-element.16), channel_id=1, source_target_pairs={{0,2},{1,3},{2,0},{3,1},{4,6},{5,7},{6,4},{7,5},{8,10},{9,11},{10,... | collective-permute-start | bytes 110600 | tf_op jit(solution)/shard_map/ppermute | solution.py:474
  6.6 3.4 %collective-permute-start.1 = (f32[48,128]{1,0:T(8,128)S(1)}, f32[48,128]{1,0:T(8,128)S(1)}, u32[]{:S(2)}, u32[]{:S(2)}) collective-permute-start(f32[48,128]{1,0:T(8,128)S(1)} %pad_maximum_fusion.2), channel_id=1, source_target_pairs={{0,10},{1,11},{2,8},{3,9},{4,14},{5,15},{6,12},{7,13},{8,2},{9,3},... | collective-permute-start | bytes 73736 | tf_op jit(solution)/shard_map/ppermute | solution.py:491
  10.0 6.4 %collective-permute-start.4 = (f32[112,128]{1,0:T(8,128)S(1)}, f32[112,128]{1,0:T(8,128)S(1)}, u32[]{:S(2)}, u32[]{:S(2)}) collective-permute-start(f32[112,128]{1,0:T(8,128)S(1)} %pad_maximum_fusion), channel_id=1, source_target_pairs={{0,3},{1,2},{2,1},{3,0},{4,7},{5,6},{6,5},{7,4},{8,11},{9,10},{10,... | collective-permute-start | bytes 172040 | tf_op jit(solution)/shard_map/ppermute | solution.py:488
  11.7 4.7 %collective-permute-start.3 = (f32[112,128]{1,0:T(8,128)S(1)}, f32[112,128]{1,0:T(8,128)S(1)}, u32[]{:S(2)}, u32[]{:S(2)}) collective-permute-start(f32[112,128]{1,0:T(8,128)S(1)} %pad_maximum_fusion), channel_id=1, source_target_pairs={{0,7},{1,6},{2,5},{3,4},{4,3},{5,2},{6,1},{7,0},{8,15},{9,14},{10,... | collective-permute-start | bytes 172040 | tf_op jit(solution)/shard_map/ppermute | solution.py:488
  13.2 4.7 %collective-permute-start.5 = (f32[96,128]{1,0:T(8,128)S(1)}, f32[96,128]{1,0:T(8,128)S(1)}, u32[]{:S(2)}, u32[]{:S(2)}) collective-permute-start(f32[96,128]{1,0:T(8,128)S(1)} %pad_maximum_fusion.1), channel_id=1, source_target_pairs={{0,6},{1,7},{2,4},{3,5},{4,2},{5,3},{6,0},{7,1},{8,14},{9,15},{10,... | collective-permute-start | bytes 147464 | tf_op jit(solution)/shard_map/ppermute | solution.py:491
  17.9 4.1 %copy-start = (f32[15]{0:T(128)S(1)}, f32[15]{0:T(128)}, u32[]{:S(2)}) copy-start(f32[15]{0:T(128)} %vdiff_ref.1) | copy-start | bytes 184
  17.9 4.9 %collective-permute-start.6 = (f32[384,128]{1,0:T(8,128)S(1)}, f32[384,128]{1,0:T(8,128)S(1)}, u32[]{:S(2)}, u32[]{:S(2)}) collective-permute-start(f32[384,128]{1,0:T(8,128)S(1)} %constant_dynamic-update-slice_fusion), channel_id=1, source_target_pairs={{0,2},{1,3},{2,0},{3,1},{4,6},{5,7},{6,4},{7,5},{8,10},{9,11},{10,... | collective-permute-start | bytes 589832 | tf_op jit(solution)/shard_map/ppermute | solution.py:494
  18.1 3.9 %collective-permute-start.7 = (f32[56,128]{1,0:T(8,128)S(1)}, f32[56,128]{1,0:T(8,128)S(1)}, u32[]{:S(2)}, u32[]{:S(2)}) collective-permute-start(f32[56,128]{1,0:T(8,128)S(1)} %get-tuple-element.17), channel_id=1, source_target_pairs={{2,4},{4,2},{3,5},{5,3},{6,8},{8,6},{7,9},{9,7},{10,12},{12,10},{1... | collective-permute-start | bytes 86024 | tf_op jit(solution)/shard_map/ppermute | solution.py:480

commit v4 on v3

--- a/solution.py
+++ b/solution.py
@@ -322,104 +322,156 @@
             out_ref[pl.ds(field * SUB, SUB), :] = jnp.where(depth > k, here + TIME_STEP * tendency, 0.0)
 
 
-def solve_kernel(
-    count, blocks, apart, own_ref, other_ref, rows_ref, surface_ref, residual_ref, rows_hbm, fields, scratch, sem
-):
+def solve_kernel(count, blocks, sources, *refs):
+    *came_refs, rows_ref, surface_ref, residual_ref, rows_hbm, fields, grids, sem = refs
     leaving = pltpu.make_async_copy(rows_ref, rows_hbm, sem)
     leaving.start()
-    me = lax.axis_index("blk") * 2 + lax.axis_index("grp")
-    height = blocks * SUB
-
-    for slot, mask in enumerate(apart):
-        fields[me ^ mask] = own_ref[slot]
-        fields[me ^ (mask ^ 2)] = other_ref[slot]
-
-    def field(part):
-        rows = slice(part * SUB, (part + 1) * SUB)
-        return tuple(
-            jnp.concatenate([fields[blk * 2 + grp, rows, :] for blk in range(blocks)], 0) for grp in range(2)
-        )
-
-    shape = (height, LANE)
-    lane = lax.broadcasted_iota(jnp.int32, shape, 1)
-    sub = tile_iota(0)
+    blk, grp = lax.axis_index("blk"), lax.axis_index("grp")
+    pitch = blocks + 1
+    halves = range(2)
+
+    first = (grp * (SUB * pitch), (1 - grp) * (SUB * pitch))
+    for ref, masks in zip(came_refs, sources):
+        for slot, mask in enumerate(masks):
+            start = first[mask & 1] + (blk ^ (mask >> 1))
+            for part in range(3):
+                at = (slot * 3 + part) * SUB
+                fields[part, pl.ds(start, SUB, stride=pitch), :] = ref[at : at + SUB, :]
+
+    def field(part, row):
+        starts = [(half * SUB + row) * pitch for half in halves]
+        return [fields[part, at : at + blocks, :] for at in starts]
+
+    residuals, applieds, alongs, easts, norths, diagonals = range(6)
+
+    def rows_of(half, row):
+        return slice((half * SUB + row) * blocks, (half * SUB + row + 1) * blocks)
+
+    def get(which, row):
+        return [grids[which, rows_of(half, row), :] for half in halves]
+
+    def put(which, row, pair):
+        for half in halves:
+            grids[which, rows_of(half, row), :] = pair[half]
+
+    def own(which):
+        return grids[which, pl.ds(grp * (SUB * blocks) + blk, SUB, stride=blocks), :]
+
+    lane = lax.broadcasted_iota(jnp.int32, (blocks, LANE), 1)
+    block = lax.broadcasted_iota(jnp.int32, (blocks, LANE), 0)
 
     def east_of(pair):
         low, high = (pltpu.roll(half, LANE - 1, 1) for half in pair)
-        return jnp.where(lane == LANE - 1, high, low), jnp.where(lane == LANE - 1, low, high)
+        return [jnp.where(lane == LANE - 1, high, low), jnp.where(lane == LANE - 1, low, high)]
 
     def west_of(pair):
         low, high = (pltpu.roll(half, 1, 1) for half in pair)
-        return jnp.where(lane == 0, high, low), jnp.where(lane == 0, low, high)
-
-    def north_of(pair, sign=1.0):
+        return [jnp.where(lane == 0, high, low), jnp.where(lane == 0, low, high)]
+
+    def above_last(lowest, highest, sign=1.0):
         out = []
-        for half, mirror in zip(pair, pair[::-1]):
-            moved = pltpu.roll(half, height - 1, 0)
-            ghost = reversed_lanes(mirror[height - SUB :, :]) * sign
-            top = jnp.where(sub == SUB - 1, ghost, moved[height - SUB :, :])
-            out.append(jnp.concatenate([moved[: height - SUB, :], top], 0))
-        return tuple(out)
-
-    def south_of(pair):
-        out = []
-        for half in pair:
-            moved = pltpu.roll(half, 1, 0)
-            bottom = jnp.where(sub == 0, 0.0, moved[:SUB, :])
-            out.append(jnp.concatenate([bottom, moved[SUB:, :]], 0))
-        return tuple(out)
-
-    u, v, depth = field(0), field(1), field(2)
-    weight_east = tuple(jnp.minimum(a, b) * (1.0 / count) for a, b in zip(depth, east_of(depth)))
-    weight_north = tuple(jnp.minimum(a, b) * (1.0 / count) for a, b in zip(depth, north_of(depth)))
-    diagonal = tuple(jnp.where(d > 0.0, SEA_DIAG, 1.0) for d in depth)
-
-    ue, uw, vn, vs = east_of(u), west_of(u), north_of(v, -1.0), south_of(v)
-    forcing = tuple(
-        jnp.where(depth[i] > 0.0, 0.5 * (ue[i] - uw[i]) + 0.5 * (vn[i] - vs[i]), 0.0) for i in range(2)
-    )
-
-    def apply_op(x):
-        xe, xn = east_of(x), north_of(x)
-        flux_e = tuple(weight_east[i] * (xe[i] - x[i]) for i in range(2))
-        flux_n = tuple(weight_north[i] * (xn[i] - x[i]) for i in range(2))
-        fw, fs = west_of(flux_e), south_of(flux_n)
-        return tuple(diagonal[i] * x[i] - (flux_e[i] - fw[i]) - (flux_n[i] - fs[i]) for i in range(2))
-
-    def total(a, b):
-        part = a[0] * b[0] + a[1] * b[1]
-        return jnp.sum(jnp.sum(part.reshape(blocks, SUB, LANE), 0), keepdims=True)
-
-    grp = me % 2
-    mine = pl.ds(pl.multiple_of((me // 2) * SUB, SUB), SUB)
-
-    def own(pair):
-        scratch[0] = pair[0]
-        scratch[1] = pair[1]
-        return jnp.where(grp == 0, scratch[0, mine, :], scratch[1, mine, :])
-
-    residual = forcing
-    applied = apply_op(residual)
-    norm_now, product = total(residual, residual), total(residual, applied)
+        for half in halves:
+            ghost = reversed_lanes(highest[1 - half][blocks - SUB :, :]) * sign
+            moved = pltpu.roll(lowest[half], blocks - 1, 0)
+            top = jnp.where(block[blocks - SUB :, :] == blocks - 1, ghost, moved[blocks - SUB :, :])
+            out.append(jnp.concatenate([moved[: blocks - SUB, :], top], 0))
+        return out
+
+    def below_first(highest):
+        return [jnp.where(block == 0, 0.0, pltpu.roll(half, 1, 0)) for half in highest]
+
+    def northward(part, sign):
+        sets = [field(part, row) for row in range(SUB)]
+        return sets, [*sets[1:], above_last(sets[0], sets[-1], sign)]
+
+    def total(value):
+        part = value[:SUB, :]
+        for at in range(SUB, blocks, SUB):
+            part = part + value[at : at + SUB, :]
+        for shift in (4, 2, 1):
+            part = part + pltpu.roll(part, shift, 0)
+        return jnp.broadcast_to(jnp.sum(part, axis=1, keepdims=True), (SUB, LANE))
+
+    def wide(value):
+        return jnp.concatenate([value] * (blocks // SUB), 0)
+
+    def apply_op(values):
+        top = above_last(values[0], values[-1])
+        squares = jnp.zeros((blocks, LANE), jnp.float32)
+        products = jnp.zeros((blocks, LANE), jnp.float32)
+
+        def north_flux(row):
+            north = values[row + 1] if row + 1 < SUB else top
+            weight = get(norths, row)
+            return [weight[half] * (north[half] - values[row][half]) for half in halves]
+
+        last = north_flux(SUB - 1)
+        flux_s = below_first(last)
+        for row in range(SUB):
+            x, weight, diagonal = values[row], get(easts, row), get(diagonals, row)
+            east = east_of(x)
+            flux_e = [weight[half] * (east[half] - x[half]) for half in halves]
+            flux_w = west_of(flux_e)
+            flux_n = north_flux(row) if row + 1 < SUB else last
+            applied = [
+                diagonal[half] * x[half] - (flux_e[half] - flux_w[half]) - (flux_n[half] - flux_s[half])
+                for half in halves
+            ]
+            put(applieds, row, applied)
+            squares += x[0] * x[0] + x[1] * x[1]
+            products += x[0] * applied[0] + x[1] * applied[1]
+            flux_s = flux_n
+        return total(squares), total(products)
+
+    depth, depth_n = northward(2, 1.0)
+    v, v_n = northward(1, -1.0)
+    v_s = below_first(v[-1])
+    forcing = []
+    for row in range(SUB):
+        here = depth[row]
+        here_e = east_of(here)
+        put(easts, row, [jnp.minimum(here[half], here_e[half]) * (1.0 / count) for half in halves])
+        put(norths, row, [jnp.minimum(here[half], depth_n[row][half]) * (1.0 / count) for half in halves])
+        put(diagonals, row, [jnp.where(here[half] > 0.0, SEA_DIAG, 1.0) for half in halves])
+        u = field(0, row)
+        u_e, u_w = east_of(u), west_of(u)
+        value = [
+            jnp.where(here[half] > 0.0, 0.5 * (u_e[half] - u_w[half]) + 0.5 * (v_n[row][half] - v_s[half]), 0.0)
+            for half in halves
+        ]
+        put(residuals, row, value)
+        forcing.append(value)
+        v_s = v[row]
+
+    norm_now, product = apply_op(forcing)
     step_len = norm_now / product
-    along = applied
-    own_residual = own(residual)
-    own_along = own(applied)
+    beta_ratio = None
+    own_residual = own(residuals)
+    own_along = own(applieds)
     own_direction = own_residual
     own_surface = jnp.zeros((SUB, LANE), jnp.float32)
     for sweep in range(ITERS):
         own_surface = own_surface + step_len * own_direction
         own_residual = own_residual - step_len * own_along
         if sweep + 1 < ITERS:
-            residual = tuple(residual[i] - step_len * along[i] for i in range(2))
-            applied = apply_op(residual)
-            norm_next, product = total(residual, residual), total(residual, applied)
+            values = []
+            wide_step = wide(step_len)
+            wide_beta = None if beta_ratio is None else wide(beta_ratio)
+            for row in range(SUB):
+                along, residual = get(applieds, row), get(residuals, row)
+                if wide_beta is not None:
+                    before = get(alongs, row)
+                    along = [along[half] + wide_beta * before[half] for half in halves]
+                value = [residual[half] - wide_step * along[half] for half in halves]
+                if sweep + 2 < ITERS:
+                    put(alongs, row, along)
+                    put(residuals, row, value)
+                values.append(value)
+            norm_next, product = apply_op(values)
             beta_ratio = norm_next / norm_now
             step_len = norm_next / (product - beta_ratio * norm_next / step_len)
             own_direction = own_residual + beta_ratio * own_direction
-            own_along = own(applied) + beta_ratio * own_along
-            if sweep + 2 < ITERS:
-                along = tuple(applied[i] + beta_ratio * along[i] for i in range(2))
+            own_along = own(applieds) + beta_ratio * own_along
             norm_now = norm_next
     surface_ref[...] = own_surface
     residual_ref[...] = own_residual
@@ -435,9 +487,8 @@
     return jax.ShapeDtypeStruct((rows, LANE), jnp.float32)
 
 
-def gather_stages(devices):
-    single = [(1 << bit | 2,) for bit in range(devices.bit_length() - 2, 2, -1)]
-    return [*single, (7, 3, 6)]
+def single_stages(devices):
+    return [1 << bit | 2 for bit in range(devices.bit_length() - 2, 2, -1)]
 
 
 def small_shards(tracers, velocity, depth_levels, vdiff):
@@ -479,19 +530,25 @@
             far_pairs += [(here, here ^ 1)] if blk == blocks - 1 else [(here, here + 2), (here + 2, here)]
     far = lax.ppermute(far, AXES, far_pairs + [(0, 1), (1, 0)])
 
-    gathered, edges, apart = sums, None, [0]
-    for masks in gather_stages(devices):
-        pieces = [gathered]
-        for mask in masks:
-            pairs = [(i, i ^ mask) for i in range(devices)]
-            if mask & 1:
-                edges = lax.ppermute(jnp.concatenate([gathered, near[halo_rows:]], 0), AXES, pairs)
-                pieces.append(edges[: gathered.shape[0]])
-            else:
-                pieces.append(lax.ppermute(gathered, AXES, pairs))
-        gathered = jnp.concatenate(pieces, 0)
-        apart = apart + [came ^ mask for mask in masks for came in apart]
-    other = lax.ppermute(gathered, AXES, [(i, i ^ 2) for i in range(devices)])
+    def exchanged(value, mask):
+        return lax.ppermute(value, AXES, [(i, i ^ mask) for i in range(devices)])
+
+    gathered, apart = sums, [0]
+    for mask in single_stages(devices):
+        gathered = jnp.concatenate([gathered, exchanged(gathered, mask)], 0)
+        apart = apart + [mask ^ came for came in apart]
+    both = exchanged(gathered, 7)
+    crossed = exchanged(jnp.concatenate([gathered, near[halo_rows:]], 0), 3)
+    second = exchanged(gathered, 6)
+    straight = exchanged(gathered, 4)
+    mine = jnp.concatenate([gathered, both, crossed[: gathered.shape[0]]], 0)
+    theirs = exchanged(mine, 2)
+    sources = (
+        [came ^ mask for mask in (0, 7, 3) for came in apart],
+        [came ^ mask ^ 2 for mask in (0, 7, 3) for came in apart],
+        [came ^ 6 for came in apart],
+        [came ^ 4 for came in apart],
+    )
 
     new_rows = pl.pallas_call(
         functools.partial(tracer_kernel, count, blocks),
@@ -500,29 +557,28 @@
         out_specs=VMEM_SPEC,
         compiler_params=SMALL_GRANT,
         name="tracer",
-    )(vdiff, tracer_rows, velocity_rows, depth, near, far, edges)
-
-    slots = devices // 2
+    )(vdiff, tracer_rows, velocity_rows, depth, near, far, crossed)
+
     surface, residual, new_rows = pl.pallas_call(
-        functools.partial(solve_kernel, count, blocks, tuple(apart)),
+        functools.partial(solve_kernel, count, blocks, sources),
         out_shape=[tile_shape(SUB), tile_shape(SUB), tile_shape(rows)],
-        in_specs=[VMEM_SPEC] * 3,
+        in_specs=[VMEM_SPEC] * 5,
         out_specs=[VMEM_SPEC, VMEM_SPEC, pl.BlockSpec(memory_space=pltpu.HBM)],
         scratch_shapes=[
-            pltpu.VMEM((devices, 3 * SUB, LANE), jnp.float32),
-            pltpu.VMEM((2, blocks * SUB, LANE), jnp.float32),
+            pltpu.VMEM((3, 2 * SUB * (blocks + 1), LANE), jnp.float32),
+            pltpu.VMEM((6, 2 * SUB * blocks, LANE), jnp.float32),
             pltpu.SemaphoreType.DMA,
         ],
         compiler_params=SMALL_GRANT,
         name="solve",
-    )(gathered.reshape(slots, 3 * SUB, LANE), other.reshape(slots, 3 * SUB, LANE), new_rows)
+    )(mine, theirs, second, straight, new_rows)
     return new_rows.reshape(tracers.shape), surface, residual
 
 
 def shards(tracers, velocity, depth_levels, vdiff):
     blocks, groups = lax.axis_size("blk"), lax.axis_size("grp")
     height, breadth = depth_levels.shape
-    tiled = (height, breadth) == (SUB, LANE) and groups == 2 and blocks >= 4 and blocks & (blocks - 1) == 0
+    tiled = (height, breadth) == (SUB, LANE) and groups == 2 and blocks >= SUB and blocks & (blocks - 1) == 0
     if tiled and 3 * tracers.shape[1] < LANE and blocks * groups * SUB * LANE <= GATHER_CELLS:
         return small_shards(tracers, velocity, depth_levels, vdiff)
     return wide_shards(tracers, velocity, depth_levels, vdiff)

time: 24.7 us -> 24.8 us (level)
  starting transfers between devices: 11.2 us -> 12.8 us
  waiting for transfers between devices: 8.91 us -> 7.46 us
    ppermute x6 -> x7, starting transfers between devices: 8.94 us -> 10.6 us  [exchanged(): return lax.ppermute(value, AXES, [(i, i ^ mask) for i in range(devices)])]
    ppermute x6 -> x7, waiting for transfers between devices: 6.53 us -> 5.12 us  [exchanged(): return lax.ppermute(value, AXES, [(i, i ^ mask) for i in range(devices)])]
  transfers between devices with their start and end apart: 8 -> 9, of which waited for: 5 -> 5; matrix products, arithmetic and copies ran while one was open for 0% -> 0% of each run, Pallas kernels for 4% -> 4%
where the time goes in v4:
time: 24.8 us; the launch traced here: 24.6 us
  starting transfers between devices  12.8 us (52%)
  waiting for transfers between devices  7.46 us (30%)
  Pallas kernels  3.62 us (15%)
  between operations  0.69 us (3%)
    ppermute x7, starting transfers between devices, exchanged(): return lax.ppermute(value, AXES, [(i, i ^ mask) for i in range(devices)])  10.6 us
    ppermute x7, waiting for transfers between devices, exchanged(): return lax.ppermute(value, AXES, [(i, i ^ mask) for i in range(devices)])  5.12 us
    ppermute x1, waiting for transfers between devices, small_shards(): far = lax.ppermute(far, AXES, far_pairs + [(0, 1), (1, 0)])  2.34 us
    pallas_call x1, Pallas kernels, small_shards(): pl.pallas_call(functools.partial(solve_kernel, count, blocks, sources), o...  1.59 us
    ppermute x1, starting transfers between devices, small_shards(): far = lax.ppermute(far, AXES, far_pairs + [(0, 1), (1, 0)])  1.53 us
    pallas_call x1, Pallas kernels, small_shards(): pl.pallas_call(functools.partial(sums_kernel, count), out_shape=[tile_sha...  1.01 us
    pallas_call x1, Pallas kernels, small_shards(): pl.pallas_call(functools.partial(tracer_kernel, count, blocks), out_shape...  0.86 us
    ppermute x1, starting transfers between devices, small_shards(): near = lax.ppermute(near, AXES, [(i, i ^ 2) for i in range(devices)])  0.74 us
  transfers between devices with their start and end apart: 9, of which 5 were waited for; matrix products, arithmetic and copies ran while one was open for 0% of the time, Pallas kernels for 4%

profile of v4, /device:TPU:0, one launch (start us, length us, event | category | flops | bytes accessed | tf_op | source)
XLA Modules:
  0.0 24.6 jit_solution(17824144032489418456)
XLA Ops:
  0.6 1.0 %sums.1 = (f32[24,128]{1,0:T(8,128)S(1)}, f32[256,128]{1,0:T(8,128)S(1)}, f32[256,128]{1,0:T(8,128)S(1)}, s32[8,128]{1,0:T(8,128)S(1)}) custom-call(f32[256,128]{1,0:T(8,128)} %bitcast.3, f32[256,128]{1,0:T(8,128)} %bitcast.4, s32[8,128]{1,0:T(8,128)} %depth_hbm.1), custom_call_target="tpu_custom_call" | custom-call | tf_op jit(solution)/shard_map/sums/pallas_call | solution.py:502
  1.6 3.6 %collective-permute-start = (f32[24,128]{1,0:T(8,128)S(1)}, f32[24,128]{1,0:T(8,128)S(1)}, u32[]{:S(2)}, u32[]{:S(2)}) collective-permute-start(f32[24,128]{1,0:T(8,128)S(1)} %get-tuple-element.12), channel_id=1, source_target_pairs={{0,18},{1,19},{2,16},{3,17},{4,22},{5,23},{6,20},{7,21},{8,26},{9,... | collective-permute-start | bytes 36872 | tf_op jit(solution)/shard_map/ppermute | solution.py:534
  5.2 0.2 pack.1
  5.4 0.7 %collective-permute-start.3 = (f32[72,128]{1,0:T(8,128)S(1)}, f32[72,128]{1,0:T(8,128)S(1)}, u32[]{:S(2)}, u32[]{:S(2)}) collective-permute-start(f32[72,128]{1,0:T(8,128)S(1)} %get-tuple-element.16), channel_id=1, source_target_pairs={{0,2},{1,3},{2,0},{3,1},{4,6},{5,7},{6,4},{7,5},{8,10},{9,11},{10,... | collective-permute-start | bytes 110600 | tf_op jit(solution)/shard_map/ppermute | solution.py:525
  6.1 0.5 %collective-permute-done = f32[24,128]{1,0:T(8,128)S(1)} collective-permute-done((f32[24,128]{1,0:T(8,128)S(1)}, f32[24,128]{1,0:T(8,128)S(1)}, u32[]{:S(2)}, u32[]{:S(2)}) %collective-permute-start) | collective-permute-done | bytes 12320 | tf_op jit(solution)/shard_map/ppermute | solution.py:534
  6.6 1.9 %collective-permute-start.1 = (f32[48,128]{1,0:T(8,128)S(1)}, f32[48,128]{1,0:T(8,128)S(1)}, u32[]{:S(2)}, u32[]{:S(2)}) collective-permute-start(f32[48,128]{1,0:T(8,128)S(1)} %pad_maximum_fusion.1), channel_id=1, source_target_pairs={{0,10},{1,11},{2,8},{3,9},{4,14},{5,15},{6,12},{7,13},{8,2},{9,3},... | collective-permute-start | bytes 73736 | tf_op jit(solution)/shard_map/ppermute | solution.py:534
  8.5 1.5 %collective-permute-done.1 = f32[48,128]{1,0:T(8,128)S(1)} collective-permute-done((f32[48,128]{1,0:T(8,128)S(1)}, f32[48,128]{1,0:T(8,128)S(1)}, u32[]{:S(2)}, u32[]{:S(2)}) %collective-permute-start.1) | collective-permute-done | bytes 24608 | tf_op jit(solution)/shard_map/ppermute | solution.py:534
  10.0 2.6 %collective-permute-start.2 = (f32[96,128]{1,0:T(8,128)S(1)}, f32[96,128]{1,0:T(8,128)S(1)}, u32[]{:S(2)}, u32[]{:S(2)}) collective-permute-start(f32[96,128]{1,0:T(8,128)S(1)} %get-tuple-element.21), channel_id=1, source_target_pairs={{0,7},{1,6},{2,5},{3,4},{4,3},{5,2},{6,1},{7,0},{8,15},{9,14},{10,... | collective-permute-start | bytes 147464 | tf_op jit(solution)/shard_map/ppermute | solution.py:534
  12.6 0.0 collective-permute-done.3.near_ref
  12.7 0.6 %collective-permute-start.4 = (f32[112,128]{1,0:T(8,128)S(1)}, f32[112,128]{1,0:T(8,128)S(1)}, u32[]{:S(2)}, u32[]{:S(2)}) collective-permute-start(f32[112,128]{1,0:T(8,128)S(1)} %pad_maximum_fusion), channel_id=1, source_target_pairs={{0,3},{1,2},{2,1},{3,0},{4,7},{5,6},{6,5},{7,4},{8,11},{9,10},{10,... | collective-permute-start | bytes 172040 | tf_op jit(solution)/shard_map/ppermute | solution.py:534
  13.3 1.5 %collective-permute-done.2 = f32[96,128]{1,0:T(8,128)S(1)} collective-permute-done((f32[96,128]{1,0:T(8,128)S(1)}, f32[96,128]{1,0:T(8,128)S(1)}, u32[]{:S(2)}, u32[]{:S(2)}) %collective-permute-start.2) | collective-permute-done | bytes 49184 | tf_op jit(solution)/shard_map/ppermute | solution.py:534
  14.8 1.6 %collective-permute-done.4.edge_ref = f32[112,128]{1,0:T(8,128)S(1)} collective-permute-done((f32[112,128]{1,0:T(8,128)S(1)}, f32[112,128]{1,0:T(8,128)S(1)}, u32[]{:S(2)}, u32[]{:S(2)}) %collective-permute-start.4) | collective-permute-done | bytes 57376 | tf_op jit(solution)/shard_map/ppermute | solution.py:534
  16.4 0.0 copy-start
  16.4 0.5 %collective-permute-start.5 = (f32[288,128]{1,0:T(8,128)S(1)}, f32[288,128]{1,0:T(8,128)S(1)}, u32[]{:S(2)}, u32[]{:S(2)}) collective-permute-start(f32[288,128]{1,0:T(8,128)S(1)} %slice_dynamic-update-slice_fusion.refs_0_), channel_id=1, source_target_pairs={{0,2},{1,3},{2,0},{3,1},{4,6},{5,7},{6,4},{7,5},{8,10},{9,11},{10,... | collective-permute-start | bytes 442376 | tf_op jit(solution)/shard_map/ppermute | solution.py:534
  16.8 0.5 %collective-permute-start.7 = (f32[96,128]{1,0:T(8,128)S(1)}, f32[96,128]{1,0:T(8,128)S(1)}, u32[]{:S(2)}, u32[]{:S(2)}) collective-permute-start(f32[96,128]{1,0:T(8,128)S(1)} %get-tuple-element.21), channel_id=1, source_target_pairs={{0,4},{1,5},{2,6},{3,7},{4,0},{5,1},{6,2},{7,3},{8,12},{9,13},{10,... | collective-permute-start | bytes 147464 | tf_op jit(solution)/shard_map/ppermute | solution.py:534
  17.3 1.0 %collective-permute-start.6 = (f32[96,128]{1,0:T(8,128)S(1)}, f32[96,128]{1,0:T(8,128)S(1)}, u32[]{:S(2)}, u32[]{:S(2)}) collective-permute-start(f32[96,128]{1,0:T(8,128)S(1)} %get-tuple-element.21), channel_id=1, source_target_pairs={{0,6},{1,7},{2,4},{3,5},{4,2},{5,3},{6,0},{7,1},{8,14},{9,15},{10,... | collective-permute-start | bytes 147464 | tf_op jit(solution)/shard_map/ppermute | solution.py:534
  18.3 1.5 %collective-permute-start.8 = (f32[56,128]{1,0:T(8,128)S(1)}, f32[56,128]{1,0:T(8,128)S(1)}, u32[]{:S(2)}, u32[]{:S(2)}) collective-permute-start(f32[56,128]{1,0:T(8,128)S(1)} %get-tuple-element.17), channel_id=1, source_target_pairs={{2,4},{4,2},{3,5},{5,3},{6,8},{8,6},{7,9},{9,7},{10,12},{12,10},{1... | collective-permute-start | bytes 86024 | tf_op jit(solution)/shard_map/ppermute | solution.py:531
  19.8 2.3 %collective-permute-done.8.far_ref = f32[56,128]{1,0:T(8,128)S(1)} collective-permute-done((f32[56,128]{1,0:T(8,128)S(1)}, f32[56,128]{1,0:T(8,128)S(1)}, u32[]{:S(2)}, u32[]{:S(2)}) %collective-permute-start.8) | collective-permute-done | bytes 28704 | tf_op jit(solution)/shard_map/ppermute | solution.py:531
  22.2 0.0 copy-done
  22.2 0.9 %tracer.1.refs_4_ = f32[256,128]{1,0:T(8,128)S(1)} custom-call(f32[15]{0:T(128)S(1)} %copy-done, f32[256,128]{1,0:T(8,128)S(1)} %get-tuple-element.13.tracers_ref, f32[256,128]{1,0:T(8,128)S(1)} %get-tuple-element.14.velocity_ref, s32[8,128]{1,0:T(8,128)S(1)} %get-tuple-element.15.depth_ref, f32[72,128]{1,0:T(8,128)S(1)} %collective-permute-done.3.near_ref, ...), custom_call_target="tpu_custom_call" | custom-call | tf_op jit(solution)/shard_map/tracer/pallas_call | solution.py:553
  23.0 0.0 collective-permute-done.7.refs_3_
  23.0 0.0 collective-permute-done.6.refs_2_
  23.0 0.0 collective-permute-done.5.refs_1_
  23.1 1.6 %solve.1 = (f32[8,128]{1,0:T(8,128)}, f32[8,128]{1,0:T(8,128)}, f32[256,128]{1,0:T(8,128)}) custom-call(f32[288,128]{1,0:T(8,128)S(1)} %slice_dynamic-update-slice_fusion.refs_0_, f32[288,128]{1,0:T(8,128)S(1)} %collective-permute-done.5.refs_1_, f32[96,128]{1,0:T(8,128)S(1)} %collective-permute-done.6.refs_2_, ...), custom_call_target="tpu_custom_call" | custom-call | tf_op jit(solution)/shard_map/solve/pallas_call | solution.py:562
  (8 shorter events, 0.0 us)
Async XLA Ops:
  1.6 5.0 %collective-permute-start = (f32[24,128]{1,0:T(8,128)S(1)}, f32[24,128]{1,0:T(8,128)S(1)}, u32[]{:S(2)}, u32[]{:S(2)}) collective-permute-start(f32[24,128]{1,0:T(8,128)S(1)} %get-tuple-element.12), channel_id=1, source_target_pairs={{0,18},{1,19},{2,16},{3,17},{4,22},{5,23},{6,20},{7,21},{8,26},{9,... | collective-permute-start | bytes 36872 | tf_op jit(solution)/shard_map/ppermute | solution.py:534
  5.4 7.3 %collective-permute-start.3 = (f32[72,128]{1,0:T(8,128)S(1)}, f32[72,128]{1,0:T(8,128)S(1)}, u32[]{:S(2)}, u32[]{:S(2)}) collective-permute-start(f32[72,128]{1,0:T(8,128)S(1)} %get-tuple-element.16), channel_id=1, source_target_pairs={{0,2},{1,3},{2,0},{3,1},{4,6},{5,7},{6,4},{7,5},{8,10},{9,11},{10,... | collective-permute-start | bytes 110600 | tf_op jit(solution)/shard_map/ppermute | solution.py:525
  6.6 3.4 %collective-permute-start.1 = (f32[48,128]{1,0:T(8,128)S(1)}, f32[48,128]{1,0:T(8,128)S(1)}, u32[]{:S(2)}, u32[]{:S(2)}) collective-permute-start(f32[48,128]{1,0:T(8,128)S(1)} %pad_maximum_fusion.1), channel_id=1, source_target_pairs={{0,10},{1,11},{2,8},{3,9},{4,14},{5,15},{6,12},{7,13},{8,2},{9,3},... | collective-permute-start | bytes 73736 | tf_op jit(solution)/shard_map/ppermute | solution.py:534
  10.0 4.7 %collective-permute-start.2 = (f32[96,128]{1,0:T(8,128)S(1)}, f32[96,128]{1,0:T(8,128)S(1)}, u32[]{:S(2)}, u32[]{:S(2)}) collective-permute-start(f32[96,128]{1,0:T(8,128)S(1)} %get-tuple-element.21), channel_id=1, source_target_pairs={{0,7},{1,6},{2,5},{3,4},{4,3},{5,2},{6,1},{7,0},{8,15},{9,14},{10,... | collective-permute-start | bytes 147464 | tf_op jit(solution)/shard_map/ppermute | solution.py:534
  12.7 3.7 %collective-permute-start.4 = (f32[112,128]{1,0:T(8,128)S(1)}, f32[112,128]{1,0:T(8,128)S(1)}, u32[]{:S(2)}, u32[]{:S(2)}) collective-permute-start(f32[112,128]{1,0:T(8,128)S(1)} %pad_maximum_fusion), channel_id=1, source_target_pairs={{0,3},{1,2},{2,1},{3,0},{4,7},{5,6},{6,5},{7,4},{8,11},{9,10},{10,... | collective-permute-start | bytes 172040 | tf_op jit(solution)/shard_map/ppermute | solution.py:534
  16.4 5.8 %copy-start = (f32[15]{0:T(128)S(1)}, f32[15]{0:T(128)}, u32[]{:S(2)}) copy-start(f32[15]{0:T(128)} %vdiff_ref.1) | copy-start | bytes 184
  16.4 6.7 %collective-permute-start.5 = (f32[288,128]{1,0:T(8,128)S(1)}, f32[288,128]{1,0:T(8,128)S(1)}, u32[]{:S(2)}, u32[]{:S(2)}) collective-permute-start(f32[288,128]{1,0:T(8,128)S(1)} %slice_dynamic-update-slice_fusion.refs_0_), channel_id=1, source_target_pairs={{0,2},{1,3},{2,0},{3,1},{4,6},{5,7},{6,4},{7,5},{8,10},{9,11},{10,... | collective-permute-start | bytes 442376 | tf_op jit(solution)/shard_map/ppermute | solution.py:534
  16.8 6.2 %collective-permute-start.7 = (f32[96,128]{1,0:T(8,128)S(1)}, f32[96,128]{1,0:T(8,128)S(1)}, u32[]{:S(2)}, u32[]{:S(2)}) collective-permute-start(f32[96,128]{1,0:T(8,128)S(1)} %get-tuple-element.21), channel_id=1, source_target_pairs={{0,4},{1,5},{2,6},{3,7},{4,0},{5,1},{6,2},{7,3},{8,12},{9,13},{10,... | collective-permute-start | bytes 147464 | tf_op jit(solution)/shard_map/ppermute | solution.py:534
  17.3 5.7 %collective-permute-start.6 = (f32[96,128]{1,0:T(8,128)S(1)}, f32[96,128]{1,0:T(8,128)S(1)}, u32[]{:S(2)}, u32[]{:S(2)}) collective-permute-start(f32[96,128]{1,0:T(8,128)S(1)} %get-tuple-element.21), channel_id=1, source_target_pairs={{0,6},{1,7},{2,4},{3,5},{4,2},{5,3},{6,0},{7,1},{8,14},{9,15},{10,... | collective-permute-start | bytes 147464 | tf_op jit(solution)/shard_map/ppermute | solution.py:534
  18.3 3.9 %collective-permute-start.8 = (f32[56,128]{1,0:T(8,128)S(1)}, f32[56,128]{1,0:T(8,128)S(1)}, u32[]{:S(2)}, u32[]{:S(2)}) collective-permute-start(f32[56,128]{1,0:T(8,128)S(1)} %get-tuple-element.17), channel_id=1, source_target_pairs={{2,4},{4,2},{3,5},{5,3},{6,8},{8,6},{7,9},{9,7},{10,12},{12,10},{1... | collective-permute-start | bytes 86024 | tf_op jit(solution)/shard_map/ppermute | solution.py:531

commit v5 on v4

--- a/solution.py
+++ b/solution.py
@@ -232,8 +232,7 @@
         far_ref[at : at + near.shape[0], :] = far
         at += near.shape[0]
     lane = tile_iota(1)
-    west_pack = jnp.zeros((SUB, LANE), jnp.float32)
-    east_pack = jnp.zeros((SUB, LANE), jnp.float32)
+    pack = jnp.zeros((SUB, LANE), jnp.float32)
     for field in range(3 * count + 1):
         if field < 2 * count:
             tile = tracers_ref[pl.ds(field * SUB, SUB), :]
@@ -241,10 +240,9 @@
             tile = velocity_ref[pl.ds((field - 2 * count) * SUB, SUB), :]
         else:
             tile = depth
-        west_pack = jnp.where(lane == field, pltpu.roll(tile, field, 1), west_pack)
-        east_pack = jnp.where(lane == field, pltpu.roll(tile, field + 1, 1), east_pack)
-    near_ref[at : at + SUB, :] = west_pack
-    near_ref[at + SUB : at + 2 * SUB, :] = east_pack
+        pack = jnp.where(lane == field, pltpu.roll(tile, field, 1), pack)
+        pack = jnp.where(lane == LANE // 2 + field, pltpu.roll(tile, LANE // 2 + field + 1, 1), pack)
+    near_ref[at : at + SUB, :] = pack
 
 
 def tracer_kernel(
@@ -262,18 +260,16 @@
     far_north = jnp.where(fold, reversed_lanes(far) * sign, far)
     north_rows = jnp.where(odd, far_north, near)
     south_rows = jnp.where(odd, near, far)
-    edge_base = edge_ref.shape[0] - 2 * SUB
-    east_cols = edge_ref[edge_base : edge_base + SUB, :]
-    west_cols = edge_ref[edge_base + SUB : edge_base + 2 * SUB, :]
-
-    def spread(packed, field, at):
-        return pltpu.roll(packed, (at - field) % LANE, 1)
+    columns = edge_ref[edge_ref.shape[0] - SUB :, :]
+
+    def spread(first, at):
+        return pltpu.roll(columns, (at - first) % LANE, 1)
 
     def east_of(tile, field):
-        return jnp.where(lane == LANE - 1, spread(east_cols, field, LANE - 1), pltpu.roll(tile, LANE - 1, 1))
+        return jnp.where(lane == LANE - 1, spread(field, LANE - 1), pltpu.roll(tile, LANE - 1, 1))
 
     def west_of(tile, field):
-        return jnp.where(lane == 0, spread(west_cols, field, 0), pltpu.roll(tile, 1, 1))
+        return jnp.where(lane == 0, spread(LANE // 2 + field, 0), pltpu.roll(tile, 1, 1))
 
     def north_of(tile, field):
         ghost = jnp.broadcast_to(north_rows[field : field + 1, :], (SUB, LANE))
@@ -515,7 +511,7 @@
     )(*(pltpu.with_memory_space_constraint(x, pltpu.HBM) for x in arguments))
     near, far = pl.pallas_call(
         functools.partial(pack_kernel, count),
-        out_shape=[tile_shape(halo_rows + 2 * SUB), tile_shape(halo_rows)],
+        out_shape=[tile_shape(halo_rows + SUB), tile_shape(halo_rows)],
         in_specs=[VMEM_SPEC] * 3,
         out_specs=[VMEM_SPEC] * 2,
         compiler_params=SMALL_GRANT,
@@ -579,7 +575,7 @@
     blocks, groups = lax.axis_size("blk"), lax.axis_size("grp")
     height, breadth = depth_levels.shape
     tiled = (height, breadth) == (SUB, LANE) and groups == 2 and blocks >= SUB and blocks & (blocks - 1) == 0
-    if tiled and 3 * tracers.shape[1] < LANE and blocks * groups * SUB * LANE <= GATHER_CELLS:
+    if tiled and 3 * tracers.shape[1] < LANE // 2 and blocks * groups * SUB * LANE <= GATHER_CELLS:
         return small_shards(tracers, velocity, depth_levels, vdiff)
     return wide_shards(tracers, velocity, depth_levels, vdiff)
 

time: 24.8 us -> 24.7 us (level)
  no operation moved by 1% of the time
where the time goes in v5:
time: 24.7 us; the launch traced here: 24.5 us
  starting transfers between devices  12.9 us (52%)
  waiting for transfers between devices  7.3 us (30%)
  Pallas kernels  3.63 us (15%)
  between operations  0.69 us (3%)
    ppermute x7, starting transfers between devices, exchanged(): return lax.ppermute(value, AXES, [(i, i ^ mask) for i in range(devices)])  10.5 us
    ppermute x7, waiting for transfers between devices, exchanged(): return lax.ppermute(value, AXES, [(i, i ^ mask) for i in range(devices)])  5.02 us
    ppermute x1, waiting for transfers between devices, small_shards(): far = lax.ppermute(far, AXES, far_pairs + [(0, 1), (1, 0)])  2.27 us
    ppermute x1, starting transfers between devices, small_shards(): far = lax.ppermute(far, AXES, far_pairs + [(0, 1), (1, 0)])  1.6 us
    pallas_call x1, Pallas kernels, small_shards(): pl.pallas_call(functools.partial(solve_kernel, count, blocks, sources), o...  1.59 us
    pallas_call x1, Pallas kernels, small_shards(): pl.pallas_call(functools.partial(sums_kernel, count), out_shape=[tile_sha...  1.01 us
    pallas_call x1, Pallas kernels, small_shards(): pl.pallas_call(functools.partial(tracer_kernel, count, blocks), out_shape...  0.86 us
    ppermute x1, starting transfers between devices, small_shards(): near = lax.ppermute(near, AXES, [(i, i ^ 2) for i in range(devices)])  0.74 us
  transfers between devices with their start and end apart: 9, of which 5 were waited for; matrix products, arithmetic and copies ran while one was open for 0% of the time, Pallas kernels for 4%

profile of v5, /device:TPU:0, one launch (start us, length us, event | category | flops | bytes accessed | tf_op | source)
XLA Modules:
  0.0 24.5 jit_solution(18233259871482331640)
XLA Ops:
  0.6 1.0 %sums.1 = (f32[24,128]{1,0:T(8,128)S(1)}, f32[256,128]{1,0:T(8,128)S(1)}, f32[256,128]{1,0:T(8,128)S(1)}, s32[8,128]{1,0:T(8,128)S(1)}) custom-call(f32[256,128]{1,0:T(8,128)} %bitcast.3, f32[256,128]{1,0:T(8,128)} %bitcast.4, s32[8,128]{1,0:T(8,128)} %depth_hbm.1), custom_call_target="tpu_custom_call" | custom-call | tf_op jit(solution)/shard_map/sums/pallas_call | solution.py:498
  1.6 3.6 %collective-permute-start = (f32[24,128]{1,0:T(8,128)S(1)}, f32[24,128]{1,0:T(8,128)S(1)}, u32[]{:S(2)}, u32[]{:S(2)}) collective-permute-start(f32[24,128]{1,0:T(8,128)S(1)} %get-tuple-element.12), channel_id=1, source_target_pairs={{0,18},{1,19},{2,16},{3,17},{4,22},{5,23},{6,20},{7,21},{8,26},{9,... | collective-permute-start | bytes 36872 | tf_op jit(solution)/shard_map/ppermute | solution.py:530
  5.2 0.2 pack.1
  5.4 0.7 %collective-permute-start.3 = (f32[64,128]{1,0:T(8,128)S(1)}, f32[64,128]{1,0:T(8,128)S(1)}, u32[]{:S(2)}, u32[]{:S(2)}) collective-permute-start(f32[64,128]{1,0:T(8,128)S(1)} %get-tuple-element.16), channel_id=1, source_target_pairs={{0,2},{1,3},{2,0},{3,1},{4,6},{5,7},{6,4},{7,5},{8,10},{9,11},{10,... | collective-permute-start | bytes 98312 | tf_op jit(solution)/shard_map/ppermute | solution.py:521
  6.1 0.5 %collective-permute-done = f32[24,128]{1,0:T(8,128)S(1)} collective-permute-done((f32[24,128]{1,0:T(8,128)S(1)}, f32[24,128]{1,0:T(8,128)S(1)}, u32[]{:S(2)}, u32[]{:S(2)}) %collective-permute-start) | collective-permute-done | bytes 12320 | tf_op jit(solution)/shard_map/ppermute | solution.py:530
  6.6 1.9 %collective-permute-start.1 = (f32[48,128]{1,0:T(8,128)S(1)}, f32[48,128]{1,0:T(8,128)S(1)}, u32[]{:S(2)}, u32[]{:S(2)}) collective-permute-start(f32[48,128]{1,0:T(8,128)S(1)} %pad_maximum_fusion.1), channel_id=1, source_target_pairs={{0,10},{1,11},{2,8},{3,9},{4,14},{5,15},{6,12},{7,13},{8,2},{9,3},... | collective-permute-start | bytes 73736 | tf_op jit(solution)/shard_map/ppermute | solution.py:530
  8.5 0.0 collective-permute-done.3.near_ref
  8.5 1.5 %collective-permute-done.1 = f32[48,128]{1,0:T(8,128)S(1)} collective-permute-done((f32[48,128]{1,0:T(8,128)S(1)}, f32[48,128]{1,0:T(8,128)S(1)}, u32[]{:S(2)}, u32[]{:S(2)}) %collective-permute-start.1) | collective-permute-done | bytes 24608 | tf_op jit(solution)/shard_map/ppermute | solution.py:530
  10.0 2.6 %collective-permute-start.2 = (f32[96,128]{1,0:T(8,128)S(1)}, f32[96,128]{1,0:T(8,128)S(1)}, u32[]{:S(2)}, u32[]{:S(2)}) collective-permute-start(f32[96,128]{1,0:T(8,128)S(1)} %get-tuple-element.21), channel_id=1, source_target_pairs={{0,7},{1,6},{2,5},{3,4},{4,3},{5,2},{6,1},{7,0},{8,15},{9,14},{10,... | collective-permute-start | bytes 147464 | tf_op jit(solution)/shard_map/ppermute | solution.py:530
  12.6 0.5 %collective-permute-start.4 = (f32[104,128]{1,0:T(8,128)S(1)}, f32[104,128]{1,0:T(8,128)S(1)}, u32[]{:S(2)}, u32[]{:S(2)}) collective-permute-start(f32[104,128]{1,0:T(8,128)S(1)} %pad_maximum_fusion), channel_id=1, source_target_pairs={{0,3},{1,2},{2,1},{3,0},{4,7},{5,6},{6,5},{7,4},{8,11},{9,10},{10,... | collective-permute-start | bytes 159752 | tf_op jit(solution)/shard_map/ppermute | solution.py:530
  13.2 1.6 %collective-permute-done.2 = f32[96,128]{1,0:T(8,128)S(1)} collective-permute-done((f32[96,128]{1,0:T(8,128)S(1)}, f32[96,128]{1,0:T(8,128)S(1)}, u32[]{:S(2)}, u32[]{:S(2)}) %collective-permute-start.2) | collective-permute-done | bytes 49184 | tf_op jit(solution)/shard_map/ppermute | solution.py:530
  14.8 1.4 %collective-permute-done.4.edge_ref = f32[104,128]{1,0:T(8,128)S(1)} collective-permute-done((f32[104,128]{1,0:T(8,128)S(1)}, f32[104,128]{1,0:T(8,128)S(1)}, u32[]{:S(2)}, u32[]{:S(2)}) %collective-permute-start.4) | collective-permute-done | bytes 53280 | tf_op jit(solution)/shard_map/ppermute | solution.py:530
  16.2 0.0 copy-start
  16.2 0.5 %collective-permute-start.5 = (f32[288,128]{1,0:T(8,128)S(1)}, f32[288,128]{1,0:T(8,128)S(1)}, u32[]{:S(2)}, u32[]{:S(2)}) collective-permute-start(f32[288,128]{1,0:T(8,128)S(1)} %slice_dynamic-update-slice_fusion.refs_0_), channel_id=1, source_target_pairs={{0,2},{1,3},{2,0},{3,1},{4,6},{5,7},{6,4},{7,5},{8,10},{9,11},{10,... | collective-permute-start | bytes 442376 | tf_op jit(solution)/shard_map/ppermute | solution.py:530
  16.7 0.5 %collective-permute-start.7 = (f32[96,128]{1,0:T(8,128)S(1)}, f32[96,128]{1,0:T(8,128)S(1)}, u32[]{:S(2)}, u32[]{:S(2)}) collective-permute-start(f32[96,128]{1,0:T(8,128)S(1)} %get-tuple-element.21), channel_id=1, source_target_pairs={{0,4},{1,5},{2,6},{3,7},{4,0},{5,1},{6,2},{7,3},{8,12},{9,13},{10,... | collective-permute-start | bytes 147464 | tf_op jit(solution)/shard_map/ppermute | solution.py:530
  17.2 1.0 %collective-permute-start.6 = (f32[96,128]{1,0:T(8,128)S(1)}, f32[96,128]{1,0:T(8,128)S(1)}, u32[]{:S(2)}, u32[]{:S(2)}) collective-permute-start(f32[96,128]{1,0:T(8,128)S(1)} %get-tuple-element.21), channel_id=1, source_target_pairs={{0,6},{1,7},{2,4},{3,5},{4,2},{5,3},{6,0},{7,1},{8,14},{9,15},{10,... | collective-permute-start | bytes 147464 | tf_op jit(solution)/shard_map/ppermute | solution.py:530
  18.1 1.6 %collective-permute-start.8 = (f32[56,128]{1,0:T(8,128)S(1)}, f32[56,128]{1,0:T(8,128)S(1)}, u32[]{:S(2)}, u32[]{:S(2)}) collective-permute-start(f32[56,128]{1,0:T(8,128)S(1)} %get-tuple-element.17), channel_id=1, source_target_pairs={{2,4},{4,2},{3,5},{5,3},{6,8},{8,6},{7,9},{9,7},{10,12},{12,10},{1... | collective-permute-start | bytes 86024 | tf_op jit(solution)/shard_map/ppermute | solution.py:527
  19.7 2.3 %collective-permute-done.8.far_ref = f32[56,128]{1,0:T(8,128)S(1)} collective-permute-done((f32[56,128]{1,0:T(8,128)S(1)}, f32[56,128]{1,0:T(8,128)S(1)}, u32[]{:S(2)}, u32[]{:S(2)}) %collective-permute-start.8) | collective-permute-done | bytes 28704 | tf_op jit(solution)/shard_map/ppermute | solution.py:527
  22.0 0.0 copy-done
  22.0 0.9 %tracer.1.refs_4_ = f32[256,128]{1,0:T(8,128)S(1)} custom-call(f32[15]{0:T(128)S(1)} %copy-done, f32[256,128]{1,0:T(8,128)S(1)} %get-tuple-element.13.tracers_ref, f32[256,128]{1,0:T(8,128)S(1)} %get-tuple-element.14.velocity_ref, s32[8,128]{1,0:T(8,128)S(1)} %get-tuple-element.15.depth_ref, f32[64,128]{1,0:T(8,128)S(1)} %collective-permute-done.3.near_ref, ...), custom_call_target="tpu_custom_call" | custom-call | tf_op jit(solution)/shard_map/tracer/pallas_call | solution.py:549
  22.9 0.0 collective-permute-done.7.refs_3_
  22.9 0.0 collective-permute-done.6.refs_2_
  22.9 0.0 collective-permute-done.5.refs_1_
  22.9 1.6 %solve.1 = (f32[8,128]{1,0:T(8,128)}, f32[8,128]{1,0:T(8,128)}, f32[256,128]{1,0:T(8,128)}) custom-call(f32[288,128]{1,0:T(8,128)S(1)} %slice_dynamic-update-slice_fusion.refs_0_, f32[288,128]{1,0:T(8,128)S(1)} %collective-permute-done.5.refs_1_, f32[96,128]{1,0:T(8,128)S(1)} %collective-permute-done.6.refs_2_, ...), custom_call_target="tpu_custom_call" | custom-call | tf_op jit(solution)/shard_map/solve/pallas_call | solution.py:558
  (8 shorter events, 0.0 us)
Async XLA Ops:
  1.6 5.0 %collective-permute-start = (f32[24,128]{1,0:T(8,128)S(1)}, f32[24,128]{1,0:T(8,128)S(1)}, u32[]{:S(2)}, u32[]{:S(2)}) collective-permute-start(f32[24,128]{1,0:T(8,128)S(1)} %get-tuple-element.12), channel_id=1, source_target_pairs={{0,18},{1,19},{2,16},{3,17},{4,22},{5,23},{6,20},{7,21},{8,26},{9,... | collective-permute-start | bytes 36872 | tf_op jit(solution)/shard_map/ppermute | solution.py:530
  5.4 3.1 %collective-permute-start.3 = (f32[64,128]{1,0:T(8,128)S(1)}, f32[64,128]{1,0:T(8,128)S(1)}, u32[]{:S(2)}, u32[]{:S(2)}) collective-permute-start(f32[64,128]{1,0:T(8,128)S(1)} %get-tuple-element.16), channel_id=1, source_target_pairs={{0,2},{1,3},{2,0},{3,1},{4,6},{5,7},{6,4},{7,5},{8,10},{9,11},{10,... | collective-permute-start | bytes 98312 | tf_op jit(solution)/shard_map/ppermute | solution.py:521
  6.6 3.4 %collective-permute-start.1 = (f32[48,128]{1,0:T(8,128)S(1)}, f32[48,128]{1,0:T(8,128)S(1)}, u32[]{:S(2)}, u32[]{:S(2)}) collective-permute-start(f32[48,128]{1,0:T(8,128)S(1)} %pad_maximum_fusion.1), channel_id=1, source_target_pairs={{0,10},{1,11},{2,8},{3,9},{4,14},{5,15},{6,12},{7,13},{8,2},{9,3},... | collective-permute-start | bytes 73736 | tf_op jit(solution)/shard_map/ppermute | solution.py:530
  10.0 4.7 %collective-permute-start.2 = (f32[96,128]{1,0:T(8,128)S(1)}, f32[96,128]{1,0:T(8,128)S(1)}, u32[]{:S(2)}, u32[]{:S(2)}) collective-permute-start(f32[96,128]{1,0:T(8,128)S(1)} %get-tuple-element.21), channel_id=1, source_target_pairs={{0,7},{1,6},{2,5},{3,4},{4,3},{5,2},{6,1},{7,0},{8,15},{9,14},{10,... | collective-permute-start | bytes 147464 | tf_op jit(solution)/shard_map/ppermute | solution.py:530
  12.6 3.6 %collective-permute-start.4 = (f32[104,128]{1,0:T(8,128)S(1)}, f32[104,128]{1,0:T(8,128)S(1)}, u32[]{:S(2)}, u32[]{:S(2)}) collective-permute-start(f32[104,128]{1,0:T(8,128)S(1)} %pad_maximum_fusion), channel_id=1, source_target_pairs={{0,3},{1,2},{2,1},{3,0},{4,7},{5,6},{6,5},{7,4},{8,11},{9,10},{10,... | collective-permute-start | bytes 159752 | tf_op jit(solution)/shard_map/ppermute | solution.py:530
  16.2 5.8 %copy-start = (f32[15]{0:T(128)S(1)}, f32[15]{0:T(128)}, u32[]{:S(2)}) copy-start(f32[15]{0:T(128)} %vdiff_ref.1) | copy-start | bytes 184
  16.2 6.7 %collective-permute-start.5 = (f32[288,128]{1,0:T(8,128)S(1)}, f32[288,128]{1,0:T(8,128)S(1)}, u32[]{:S(2)}, u32[]{:S(2)}) collective-permute-start(f32[288,128]{1,0:T(8,128)S(1)} %slice_dynamic-update-slice_fusion.refs_0_), channel_id=1, source_target_pairs={{0,2},{1,3},{2,0},{3,1},{4,6},{5,7},{6,4},{7,5},{8,10},{9,11},{10,... | collective-permute-start | bytes 442376 | tf_op jit(solution)/shard_map/ppermute | solution.py:530
  16.7 6.2 %collective-permute-start.7 = (f32[96,128]{1,0:T(8,128)S(1)}, f32[96,128]{1,0:T(8,128)S(1)}, u32[]{:S(2)}, u32[]{:S(2)}) collective-permute-start(f32[96,128]{1,0:T(8,128)S(1)} %get-tuple-element.21), channel_id=1, source_target_pairs={{0,4},{1,5},{2,6},{3,7},{4,0},{5,1},{6,2},{7,3},{8,12},{9,13},{10,... | collective-permute-start | bytes 147464 | tf_op jit(solution)/shard_map/ppermute | solution.py:530
  17.2 5.7 %collective-permute-start.6 = (f32[96,128]{1,0:T(8,128)S(1)}, f32[96,128]{1,0:T(8,128)S(1)}, u32[]{:S(2)}, u32[]{:S(2)}) collective-permute-start(f32[96,128]{1,0:T(8,128)S(1)} %get-tuple-element.21), channel_id=1, source_target_pairs={{0,6},{1,7},{2,4},{3,5},{4,2},{5,3},{6,0},{7,1},{8,14},{9,15},{10,... | collective-permute-start | bytes 147464 | tf_op jit(solution)/shard_map/ppermute | solution.py:530
  18.1 3.9 %collective-permute-start.8 = (f32[56,128]{1,0:T(8,128)S(1)}, f32[56,128]{1,0:T(8,128)S(1)}, u32[]{:S(2)}, u32[]{:S(2)}) collective-permute-start(f32[56,128]{1,0:T(8,128)S(1)} %get-tuple-element.17), channel_id=1, source_target_pairs={{2,4},{4,2},{3,5},{5,3},{6,8},{8,6},{7,9},{9,7},{10,12},{12,10},{1... | collective-permute-start | bytes 86024 | tf_op jit(solution)/shard_map/ppermute | solution.py:527
